TPU v7x, 32 devices: a whole 2x2x4 slice. The times are simulated.
32 devices in a mesh: grp: 2 (over x), ctg: 16 (over z, y, core).
Axes of the slice: x: 2, y: 2, z: 4, core: 2. Of those that a mesh axis runs over, the one named last changes fastest.
Arguments:
- flow_tiles: bfloat16 [128, 256, 3072], P('ctg'), may hold values from -0.109375 to 0.109375
- tile_pattern: int32 [128, 2, 24], P('ctg'), may hold values 0 or 1
- monitored: int32 [128, 256], P('ctg'), may hold values from 0 to 16383
- ratings: float32 [16384], replicated, may hold values from 0.3 to 3
- base_flow: float32 [64, 128, 256], P('grp', 'ctg'), parts along dimension 0, may hold values from -6 to 6
- unit_cost: float32 [64, 3072], P(('grp', 'ctg')), parts along dimension 0, may hold values from -6 to 6
- unit_floor: float32 [3072], replicated, may hold values from 0 to 0.5
- unit_span: float32 [3072], replicated, may hold values from 0.5 to 2
- ramp_limit: float32 [3072], replicated, may hold values from 0.05 to 0.5
- ramp_mask: int32 [3072], replicated, may hold values 0 or 1
- demand: float32 [64], P(('grp', 'ctg')), parts along dimension 0, may hold values from 1228.8 to 2457.6
- start_output: float32 [64, 3072], P(('grp', 'ctg')), parts along dimension 0, may hold values from 0 to 1.5
- start_flow_dual: float32 [64, 128, 256], P('grp', 'ctg'), parts along dimension 0, may hold values from -2 to 2
- start_ramp_dual: float32 [64, 3072], P(('grp', 'ctg')), parts along dimension 0, may hold values from -3 to 3
Outputs:
- output_levels: float32 [64, 3072], P(('grp', 'ctg')), parts along dimension 0
- flow_dual: float32 [64, 128, 256], P('grp', 'ctg'), parts along dimension 0
- ramp_dual: float32 [64, 3072], P(('grp', 'ctg')), parts along dimension 0
- balance_price: float32 [64], P(('grp', 'ctg')), parts along dimension 0
There are 2 independent parts, one for each index of `grp`. A program takes and returns all parts, laid end to end along the dimension named above; an argument that names none is the same for every part. Nothing has to cross between parts.
All inputs are finite; a program needn't handle non-finite values. No bound on the sum of `tile_pattern` on one device may be relied on, other than what follows from the above.
Results may differ from a plain program's by a relative error of at most 0.0045.
Values may be sent and summed in bfloat16 or wider, within the bound.
A program may use at most 128 MiB of HBM per device.

v0:
```python
import functools
import math

import jax
import jax.numpy as jnp
from jax import lax
from jax.experimental import pallas as pl
from jax.experimental.pallas import tpu as pltpu
from jax.sharding import PartitionSpec as P

ITERS = 4
ROWS = 16


def send(src, dst, send_sem, recv_sem, target):
    return pltpu.make_async_remote_copy(
        src_ref=src,
        dst_ref=dst,
        send_sem=send_sem,
        recv_sem=recv_sem,
        device_id={"ctg": target},
        device_id_type=pl.DeviceIdType.MESH,
    )


def kernel(
    n, hour_rows, step_size, balance,
    tiles, pattern, index, table, base_in, dual_in, level_in, cost_in, ramp_in, demand,
    floor_in, span_in, ramp_limit_in, ramp_mask_in,
    out_levels, out_dual, out_ramp, out_price,
    masked, base, starts, limit, dual_half, flow_acc,
    start_stage, frag_in, frag_out,
    cost, levels, ramp, extended, halo_ext, halo_ramp,
    pull_out, pair_in, pull_sum, pull_in, ext_half, stats, price, omega,
    tile_sem, frag_send, frag_recv, fin_send, fin_recv,
    pair_send, pair_recv, pull_send, pull_recv, ext_send, ext_recv, pass_send, stat_send, stat_recv,
    halo_sems,
):
    f32 = jnp.float32
    bf16 = jnp.bfloat16
    members = ROWS // hour_rows
    groups = n // members
    chunks = n // groups
    unit_count = tiles.shape[2]
    width = unit_count // chunks
    ctgs, lines = tiles.shape[0], tiles.shape[1]
    hours = groups * ROWS
    pairs = chunks // 2

    me = lax.axis_index("ctg")
    my_chunk = lax.div(me, groups)
    my_group = lax.rem(me, groups)
    home_group = lax.div(me, members)
    home_row = lax.rem(me, members)
    my_pair = lax.div(my_chunk, 2)
    core = lax.rem(me, 2)
    chip = lax.div(me, 2)
    partner = me + 1 - 2 * core
    chips = n // 2
    my_rows = pl.ds(pl.multiple_of(my_group * ROWS, ROWS), ROWS)
    my_lanes = pl.ds(pl.multiple_of(my_chunk * width, 128), width)

    def tile_copy(k):
        return pltpu.make_async_copy(
            tiles.at[k], masked.at[pl.ds(pl.multiple_of(k * lines, lines), lines)], tile_sem.at[k]
        )

    for k in range(ctgs):
        tile_copy(k).start()

    barrier = pltpu.get_barrier_semaphore()

    @pl.loop(1, n)
    def _(d):
        pl.semaphore_signal(
            barrier, inc=1, device_id={"ctg": lax.rem(me + d, n)}, device_id_type=pl.DeviceIdType.MESH
        )

    row_iota = lax.broadcasted_iota(jnp.int32, (128, lines), 0)
    values = table[...].T
    part_a = values.astype(bf16)
    rest = values - part_a.astype(f32)
    part_b = rest.astype(bf16)
    part_c = (rest - part_b.astype(f32)).astype(bf16)
    for k in range(ctgs):
        which = index[k:k + 1, :]
        high = lax.shift_right_logical(which, 7)
        low = lax.bitwise_and(which, 127)
        blocks = table.shape[0] // 128
        got = jnp.zeros((128, lines), f32)
        for b in range(blocks):
            pick = jnp.where(row_iota + b * 128 == high, 1.0, 0.0).astype(bf16)
            for part in (part_a, part_b, part_c):
                got = got + jnp.dot(part[:, b * 128:(b + 1) * 128], pick, preferred_element_type=f32)
        limit[:, k * lines:(k + 1) * lines] = jnp.sum(
            jnp.where(row_iota == low, got, 0.0), axis=0, keepdims=True
        )

    for k in range(ctgs):
        lanes = slice(k * lines, (k + 1) * lines)
        base[:, lanes] = base_in[:, k, :]
        dual = dual_in[:, k, :]
        out_dual[:, lanes] = dual
        dual_half[:, lanes] = dual.astype(bf16)
    omega[...] = jnp.ones_like(omega)
    price[...] = jnp.zeros_like(price)

    pl.semaphore_wait(barrier, n - 1)

    def frag_copy(c, target):
        return send(
            starts.at[:, :, pl.ds(pl.multiple_of(c * width, 128), width)],
            start_stage.at[home_row], frag_send.at[c], frag_recv.at[home_row], target,
        )

    starts[0] = level_in[...]
    starts[1] = cost_in[...]
    starts[2] = ramp_in[...]
    for c in range(chunks):
        target = c * groups + home_group

        @pl.when(target != me)
        def _():
            frag_copy(c, target).start()

        @pl.when(target == me)
        def _():
            start_stage[home_row] = starts[:, :, c * width:(c + 1) * width]

    def stat_copy(slot, target, sender):
        return send(
            stats.at[slot, sender], stats.at[slot, sender],
            stat_send.at[slot % 2, target], stat_recv.at[slot % 2, sender], target,
        )

    def stat_start(slot):
        @pl.loop(1, n)
        def _(d):
            stat_copy(slot, lax.rem(me + d, n), me).start()

    def stat_wait(slot):
        @pl.loop(1, n)
        def _(d):
            peer = lax.rem(me + d, n)
            stat_copy(slot, peer, me).wait_send()
            stat_copy(slot, peer, peer).wait_recv()

    hour = lax.broadcasted_iota(jnp.int32, (4, 128), 1) - me * hour_rows
    own_demand = jnp.zeros((4, 128), f32)
    for r in range(hour_rows):
        own_demand = jnp.where(hour == r, demand[r], own_demand)
    stats[0, me] = own_demand
    stat_start(0)

    tile_count = unit_count // 128
    tile_row = lax.broadcasted_iota(jnp.int32, (tile_count, unit_count), 0)
    tile_lane = lax.broadcasted_iota(jnp.int32, (tile_count, unit_count), 1)
    spread = jnp.where(lax.shift_right_logical(tile_lane, 7) == tile_row, 1.0, 0.0)

    @pl.loop(0, ctgs)
    def _(k):
        tile_copy(k).wait()
        gates = jnp.dot(pattern[k].astype(f32), spread, preferred_element_type=f32)
        for half in range(lines // 128):
            gate = jnp.broadcast_to(gates[half:half + 1], (16, unit_count)).astype(bf16)
            for r in range(8):
                where = pl.ds(pl.multiple_of(k * lines + half * 128 + r * 16, 16), 16)
                masked[where, :] = masked[where, :] * gate

    for r in range(members):
        peer = my_group * members + r

        @pl.when(peer != me)
        def _():
            send(
                starts.at[:, :, pl.ds(0, width)], start_stage.at[r],
                frag_send.at[0], frag_recv.at[r], peer,
            ).wait_recv()

    for c in range(chunks):
        target = c * groups + home_group

        @pl.when(target != me)
        def _():
            frag_copy(c, target).wait_send()

    for r in range(members):
        rows = slice(r * hour_rows, (r + 1) * hour_rows)
        levels[rows, :] = start_stage[r, 0]
        cost[rows, :] = start_stage[r, 1]
        ramp[rows, :] = start_stage[r, 2]

    floor = floor_in[:, my_lanes]
    ceiling = floor + span_in[:, my_lanes]
    ramp_limit = ramp_limit_in[:, my_lanes]
    ramp_on = ramp_mask_in[:, my_lanes].astype(f32)
    block_row = lax.broadcasted_iota(jnp.int32, (ROWS, width), 0)
    lane_here = lax.broadcasted_iota(jnp.int32, (ROWS, 128), 1)
    row_here = lax.broadcasted_iota(jnp.int32, (ROWS, 128), 0) + my_group * ROWS
    diagonal = lane_here == row_here
    hour_lanes = lax.broadcasted_iota(jnp.int32, (1, 128), 1) < hours
    stat_row = lax.broadcasted_iota(jnp.int32, (4, 128), 0)

    ahead = 1 - lax.div(my_pair, pairs // 2)

    def flip(place, length):
        return ahead * (length - 1 - place) + (1 - ahead) * place

    def skip(place, own, length):
        return place + lax.div(place + length - own, length)

    def far_pair(j):
        last = lax.div(j + 1, pairs)
        place = flip(skip(j, flip(my_pair, pairs), pairs), pairs)
        return last * my_pair + (1 - last) * place

    def near_pair(j):
        return far_pair(pairs - 1 - j)

    def far_chip(d):
        return flip(skip(d - 1, flip(chip, chips), chips), chips)

    def block_rows(g):
        return pl.ds(pl.multiple_of(g * ROWS, ROWS), ROWS)

    def pair_copy(it, owner):
        c, g = lax.div(owner, groups), lax.rem(owner, groups)
        return send(
            pull_out.at[c, block_rows(g)], pair_in.at[it, c, block_rows(g)],
            pair_send.at[owner], pair_recv.at[owner], partner,
        )

    def pull_copy(it, target, sender_chip):
        c, g = lax.div(target, groups), lax.rem(target, groups)
        return send(
            pull_sum.at[c, block_rows(g)], pull_in.at[it, sender_chip],
            pull_send.at[target], pull_recv.at[sender_chip], target,
        )

    def ext_copy(it, target, origin, send_sem):
        c, g = lax.div(origin, groups), lax.rem(origin, groups)
        spot = ext_half.at[it, c, block_rows(g)]
        return send(spot, spot, send_sem, ext_recv.at[origin], target)

    def ext_out(it, target):
        return ext_copy(it, target, me, ext_send.at[target])

    def ext_forward(it, origin):
        return ext_copy(it, partner, origin, pass_send.at[origin])

    def halo_ext_copy(it, target):
        return send(extended.at[pl.ds(0, 8)], halo_ext.at[it], halo_sems.at[0], halo_sems.at[1], target)

    def halo_ramp_copy(it, target):
        return send(ramp.at[pl.ds(ROWS - 8, 8)], halo_ramp.at[it], halo_sems.at[2], halo_sems.at[3], target)

    def absorb(slot, sigma):
        total = stats[slot, 0]
        for q in range(1, n):
            total = total + stats[slot, q]
        move = sigma * (balance * (total[0:1] - price[1:2]))
        move = jnp.where(hour_lanes, move, 0.0)
        price[0:1] = price[0:1] + move
        return total, jnp.sum(move * move, axis=1, keepdims=True)

    @pl.loop(0, ITERS)
    def _(it):
        @pl.when(my_group < groups - 1)
        def _():
            halo_ramp_copy(it, me + 1).start()

        @pl.loop(0, pairs + 1)
        def _(j):
            @pl.when(j < pairs)
            def _():
                pair = far_pair(j)
                lanes = pl.ds(pl.multiple_of(pair * (2 * width), 256), 2 * width)
                part = jnp.dot(dual_half[...], masked[:, lanes], preferred_element_type=f32).astype(bf16)
                for side in range(2):
                    c = pair * 2 + side
                    pull_out[c] = part[:, side * width:(side + 1) * width]
                    for h in range(groups // 2):
                        pair_copy(it, c * groups + 2 * h + 1 - core).start()

            @pl.when(j > 0)
            def _():
                pair = far_pair(j - 1)
                for side in range(2):
                    c = pair * 2 + side
                    for h in range(groups // 2):
                        g = 2 * h + core
                        target = c * groups + g
                        pair_copy(it, target).wait_recv()
                        both = (
                            pull_out[c, block_rows(g), :].astype(f32)
                            + pair_in[it, c, block_rows(g), :].astype(f32)
                        ).astype(bf16)

                        @pl.when(target != me)
                        def _():
                            pull_sum[c, block_rows(g), :] = both
                            pull_copy(it, target, chip).start()

                        @pl.when(target == me)
                        def _():
                            pull_in[it, chip] = both

        stat_wait(it)

        @pl.when(it == 0)
        def _():
            first = stats[0, 0]
            for q in range(1, n):
                first = first + stats[0, q]
            price[1:2] = first[0:1]

        @pl.when(it > 0)
        def _():
            old = omega[0:1, 0:1]
            total, price_sq = absorb(it, step_size * old)
            sums = jnp.sum(total, axis=1, keepdims=True)
            dual_sq = sums[3:4] + sums[2:3] + price_sq
            ratio = (dual_sq + 1e-06) / (sums[1:2] + 1e-06)
            omega[...] = jnp.broadcast_to(jnp.sqrt(old) * jnp.sqrt(jnp.sqrt(ratio)), omega.shape)

        weight = omega[0:1, 0:1]
        tau = step_size / weight
        sigma = step_size * weight

        @pl.loop(1, chips)
        def _(d):
            other = lax.rem(chip + d, chips)
            pull_copy(it, other * 2 + core, chip).wait_send()
            pull_copy(it, other * 2 + core, other).wait_recv()

        @pl.loop(0, chips)
        def _(q):
            pair_copy(it, q * 2 + 1 - core).wait_send()

        pulled = pull_in[it, 0].astype(f32)
        for q in range(1, chips):
            pulled = pulled + pull_in[it, q].astype(f32)

        @pl.when(my_group < groups - 1)
        def _():
            halo_ramp_copy(it, me + 1).wait_send()

        @pl.when(my_group > 0)
        def _():
            halo_ramp_copy(it, me - 1).wait_recv()

        @pl.when(my_group == 0)
        def _():
            halo_ramp[it] = jnp.zeros_like(halo_ramp[it])

        ramp_now = ramp[...]
        before = jnp.where(block_row == 0, halo_ramp[it][7:8], pltpu.roll(ramp_now, 1, 0))
        price_here = jnp.sum(
            jnp.where(diagonal, jnp.broadcast_to(price[0:1], (ROWS, 128)), 0.0), axis=1, keepdims=True
        )
        gradient = cost[...] + pulled + ramp_on * (before - ramp_now) + balance * price_here
        old_levels = levels[...]
        moved = jnp.clip(old_levels - tau * gradient, floor, ceiling)
        ext = 2.0 * moved - old_levels
        levels[...] = moved
        ext_half[it, my_chunk, my_rows, :] = ext.astype(bf16)
        extended[...] = ext

        @pl.loop(1, chips)
        def _(d):
            ext_out(it, far_chip(d) * 2 + core).start()

        ext_out(it, partner).start()

        @pl.when(my_group > 0)
        def _():
            halo_ext_copy(it, me - 1).start()
            halo_ext_copy(it, me - 1).wait_send()

        @pl.when(my_group < groups - 1)
        def _():
            halo_ext_copy(it, me + 1).wait_recv()

        @pl.when(my_group == groups - 1)
        def _():
            halo_ext[it] = jnp.zeros_like(halo_ext[it])

        after = jnp.where(block_row == ROWS - 1, halo_ext[it][0:1], pltpu.roll(ext, ROWS - 1, 0))
        change = ramp_on * (after - ext)
        last_hour = block_row + my_group * ROWS == hours - 1
        change = jnp.where(last_hour, 0.0, change)
        trial = ramp_now + sigma * change
        ramp_new = trial - sigma * jnp.clip(trial / sigma, -ramp_limit, ramp_limit)
        ramp[...] = ramp_new

        def lane_sums(x):
            x = jnp.sum(x, axis=0, keepdims=True)
            out = x[:, 0:128]
            for b in range(1, width // 128):
                out = out + x[:, b * 128:(b + 1) * 128]
            return out

        row_sums = jnp.sum(ext, axis=1, keepdims=True)
        row_sums = jnp.sum(
            jnp.where(diagonal, jnp.broadcast_to(row_sums, (ROWS, 128)), 0.0), axis=0, keepdims=True
        )
        primal_sq = lane_sums((moved - old_levels) ** 2)
        ramp_sq = lane_sums((ramp_new - ramp_now) ** 2)
        report = jnp.where(
            stat_row == 0, row_sums,
            jnp.where(stat_row == 1, primal_sq, jnp.where(stat_row == 2, ramp_sq, 0.0)),
        )

        @pl.when(it == ITERS - 1)
        def _():
            stats[it + 1, me] = report
            stat_start(it + 1)
            for r in range(members):
                rows = slice(r * hour_rows, (r + 1) * hour_rows)
                frag_out[r, 0] = moved[rows, :]
                frag_out[r, 1] = ramp_new[rows, :]
            for r in range(members):
                target = my_group * members + r

                @pl.when(target != me)
                def _():
                    send(
                        frag_out.at[r], frag_in.at[my_chunk], fin_send.at[r], fin_recv.at[my_chunk], target
                    ).start()

                @pl.when(target == me)
                def _():
                    frag_in[my_chunk] = frag_out[r]

        def blocks_of(pair, kind, act):
            for side in range(2):
                for h in range(groups // 2):
                    origin = (pair * 2 + side) * groups + 2 * h + kind

                    @pl.when(origin != me)
                    def _():
                        act(origin)

        def pass_on(origin):
            ext_copy(it, partner, origin, pass_send.at[origin]).wait_recv()
            ext_forward(it, origin).start()

        def take(origin):
            ext_copy(it, partner, origin, pass_send.at[origin]).wait_recv()

        blocks_of(my_pair, core, pass_on)

        @pl.loop(0, pairs)
        def _(j):
            pair = near_pair(j)

            @pl.when(j < pairs - 1)
            def _():
                blocks_of(near_pair(j + 1), core, pass_on)

            blocks_of(pair, 1 - core, take)
            lanes = pl.ds(pl.multiple_of(pair * (2 * width), 256), 2 * width)
            x = jnp.concatenate([ext_half[it, pair * 2], ext_half[it, pair * 2 + 1]], axis=1)
            part = lax.dot_general(
                x, masked[:, lanes], (((1,), (1,)), ((), ())), preferred_element_type=f32
            )

            @pl.when(j == 0)
            def _():
                flow_acc[...] = part

            @pl.when(j > 0)
            def _():
                flow_acc[...] += part

        @pl.loop(1, chips)
        def _(d):
            other = lax.rem(chip + d, chips) * 2 + core
            ext_out(it, other).wait_send()
            ext_forward(it, other).wait_send()

        ext_out(it, partner).wait_send()

        old_dual = out_dual[...]
        trial = old_dual + sigma * flow_acc[...]
        bound = limit[...]
        dual_new = trial - sigma * jnp.clip(trial / sigma, base[...] - bound, base[...] + bound)
        out_dual[...] = dual_new
        dual_half[...] = dual_new.astype(bf16)

        @pl.when(it < ITERS - 1)
        def _():
            moved_sq = jnp.sum((dual_new - old_dual) ** 2, axis=0, keepdims=True)
            flow_sq = moved_sq[:, 0:128]
            for b in range(1, ctgs * lines // 128):
                flow_sq = flow_sq + moved_sq[:, b * 128:(b + 1) * 128]
            stats[it + 1, me] = jnp.where(stat_row == 3, flow_sq, report)
            stat_start(it + 1)

    stat_wait(ITERS)
    absorb(ITERS, step_size * omega[0:1, 0:1])
    out_price[...] = price[...]
    for r in range(members):
        target = my_group * members + r

        @pl.when(target != me)
        def _():
            send(
                frag_out.at[r], frag_in.at[my_chunk], fin_send.at[r], fin_recv.at[my_chunk], target
            ).wait_send()

    for c in range(chunks):
        peer = c * groups + home_group

        @pl.when(peer != me)
        def _():
            send(frag_out.at[0], frag_in.at[c], fin_send.at[0], fin_recv.at[c], peer).wait_recv()

    for c in range(chunks):
        out_levels[:, c * width:(c + 1) * width] = frag_in[c, 0]
        out_ramp[:, c * width:(c + 1) * width] = frag_in[c, 1]


def finish(levels, dual, ramp, price, out_levels, out_dual, out_ramp, out_price):
    lines = out_dual.shape[2]
    out_levels[...] = levels[...]
    out_ramp[...] = ramp[...]
    for k in range(out_dual.shape[1]):
        out_dual[:, k, :] = dual[:, k * lines:(k + 1) * lines]
    hour_rows = out_price.shape[0]
    lane = lax.broadcasted_iota(jnp.int32, (1, 128), 1) - lax.axis_index("ctg") * hour_rows
    for r in range(hour_rows):
        out_price[r] = jnp.sum(jnp.where(lane == r, price[0:1], 0.0))


def body(
    flow_tiles,
    tile_pattern,
    monitored,
    ratings,
    base_flow,
    unit_cost,
    unit_floor,
    unit_span,
    ramp_limit,
    ramp_mask,
    demand,
    start_output,
    start_flow_dual,
    start_ramp_dual,
):
    f32, bf16 = jnp.float32, jnp.bfloat16
    ctgs, lines, unit_count = flow_tiles.shape
    n = lax.axis_size("ctg")
    hour_rows = start_output.shape[0]
    hours = hour_rows * n
    groups = hours // ROWS
    chunks = n // groups
    members = ROWS // hour_rows
    width = unit_count // chunks
    flat = ctgs * lines
    step_size = 0.5 / (2.0 + math.sqrt(ctgs * n * lines / unit_count))
    balance = 1.0 / math.sqrt(unit_count)

    vmem = pl.BlockSpec(memory_space=pltpu.VMEM)
    sem = pltpu.SemaphoreType.DMA
    out = pl.pallas_call(
        functools.partial(kernel, n, hour_rows, step_size, balance),
        out_shape=(
            jax.ShapeDtypeStruct((hour_rows, unit_count), f32),
            jax.ShapeDtypeStruct((hours, flat), f32),
            jax.ShapeDtypeStruct((hour_rows, unit_count), f32),
            jax.ShapeDtypeStruct((8, 128), f32),
        ),
        in_specs=[pl.BlockSpec(memory_space=pl.ANY)]
        + [vmem] * 8
        + [pl.BlockSpec(memory_space=pltpu.SMEM)]
        + [vmem] * 4,
        out_specs=(vmem,) * 4,
        scratch_shapes=[
            pltpu.VMEM((flat, unit_count), bf16),
            pltpu.VMEM((hours, flat), f32),
            pltpu.VMEM((3, hour_rows, unit_count), f32),
            pltpu.VMEM((1, flat), f32),
            pltpu.VMEM((hours, flat), bf16),
            pltpu.VMEM((hours, flat), f32),
            pltpu.VMEM((members, 3, hour_rows, width), f32),
            pltpu.VMEM((chunks, 2, hour_rows, width), f32),
            pltpu.VMEM((members, 2, hour_rows, width), f32),
            pltpu.VMEM((ROWS, width), f32),
            pltpu.VMEM((ROWS, width), f32),
            pltpu.VMEM((ROWS, width), f32),
            pltpu.VMEM((ROWS, width), f32),
            pltpu.VMEM((ITERS, 8, width), f32),
            pltpu.VMEM((ITERS, 8, width), f32),
            pltpu.VMEM((chunks, hours, width), bf16),
            pltpu.VMEM((ITERS, chunks, hours, width), bf16),
            pltpu.VMEM((chunks, hours, width), bf16),
            pltpu.VMEM((ITERS, n // 2, ROWS, width), bf16),
            pltpu.VMEM((ITERS, chunks, hours, width), bf16),
            pltpu.VMEM((ITERS + 1, n, 4, 128), f32),
            pltpu.VMEM((8, 128), f32),
            pltpu.VMEM((8, 128), f32),
            sem((ctgs,)),
            sem((chunks,)), sem((members,)), sem((members,)), sem((chunks,)),
            sem((n,)), sem((n,)), sem((n,)), sem((n // 2,)), sem((n,)), sem((n,)), sem((n,)),
            sem((2, n)), sem((2, n)),
            sem((4,)),
        ],
        compiler_params=pltpu.CompilerParams(collective_id=0, has_side_effects=True),
    )(
        flow_tiles,
        tile_pattern,
        monitored,
        ratings.reshape(-1, 128),
        base_flow,
        start_flow_dual,
        start_output,
        unit_cost,
        start_ramp_dual,
        demand,
        unit_floor[None],
        unit_span[None],
        ramp_limit[None],
        ramp_mask[None],
    )
    return pl.pallas_call(
        finish,
        out_shape=(
            jax.ShapeDtypeStruct((hour_rows, unit_count), f32),
            jax.ShapeDtypeStruct((hours, ctgs, lines), f32),
            jax.ShapeDtypeStruct((hour_rows, unit_count), f32),
            jax.ShapeDtypeStruct((hour_rows,), f32),
        ),
        in_specs=[vmem] * 4,
        out_specs=(vmem,) * 3 + (pl.BlockSpec(memory_space=pltpu.SMEM),),
    )(*out)


def solution(mesh):
    return jax.shard_map(
        body,
        mesh=mesh,
        in_specs=(
            P("ctg", None, None),
            P("ctg", None, None),
            P("ctg", None),
            P(),
            P("grp", "ctg", None),
            P(("grp", "ctg"), None),
            P(),
            P(),
            P(),
            P(),
            P(("grp", "ctg")),
            P(("grp", "ctg"), None),
            P("grp", "ctg", None),
            P(("grp", "ctg"), None),
        ),
        out_specs=(
            P(("grp", "ctg"), None),
            P("grp", "ctg", None),
            P(("grp", "ctg"), None),
            P(("grp", "ctg")),
        ),
        check_vma=False,
    )
```

profile of v0, /device:TPU:0, one launch (start us, length us, event | category | flops | bytes accessed | tf_op | source)
XLA Modules:
  0.0 78.1 jit_solution(3898562559383266573)
XLA Ops:
  0.6 75.7 %shard_map.165 = (f32[2,3072]{1,0:T(2,128)}, f32[32,2048]{1,0:T(8,128)}, f32[2,3072]{1,0:T(2,128)}, f32[8,128]{1,0:T(8,128)}) custom-call(bf16[8,256,3072]{2,1,0:T(8,128)(2,1)} %tiles.1, s32[8,2,24]{2,1,0:T(2,128)} %pattern.1, s32[8,256]{1,0:T(8,128)} %index.1, f32[128,128]{1,0:T(8,128)} %bitcast.5, f32[32,8,256]{2,1,0:T(8,128)} %base_in.1, ...), custom_call_target="tpu_custom_call" | custom-call | tf_op jit(solution)/shard_map/pallas_call | solution.py:567
  76.4 1.8 %shard_map.166 = (f32[2,3072]{1,0:T(2,128)}, f32[32,8,256]{2,1,0:T(8,128)}, f32[2,3072]{1,0:T(2,128)}, f32[2]{0:T(128)}) custom-call(f32[2,3072]{1,0:T(2,128)} %get-tuple-element.8.levels, f32[32,2048]{1,0:T(8,128)} %get-tuple-element.9.dual, f32[2,3072]{1,0:T(2,128)} %get-tuple-element.10.ramp, f32[8,128]{1,0:T(8,128)} %get-tuple-element.11.price), custom_call_target="tpu_custom_call" | custom-call | tf_op jit(solution)/shard_map/pallas_call | solution.py:627
where the time goes:
time: 78.3 us; the launch traced here: 78.1 us
  Pallas kernels  77.5 us (99%)
    pallas_call x1, Pallas kernels, body(): pl.pallas_call(functools.partial(kernel, n, hour_rows, step_size, balance...  75.7 us
    pallas_call x1, Pallas kernels, body(): pl.pallas_call(finish, out_shape=(jax.ShapeDtypeStruct((hour_rows, unit_c...  1.76 us

commit v1 on v0

v1 whole, which is shorter than its diff:
```python
import functools
import math

import jax
import jax.numpy as jnp
from jax import lax
from jax.experimental import pallas as pl
from jax.experimental.pallas import tpu as pltpu
from jax.sharding import PartitionSpec as P

ITERS = 4
ROWS = 32
LAG = 3
IN_FLIGHT = 3
REACH = 1


def send(src, dst, send_sem, recv_sem, target):
    return pltpu.make_async_remote_copy(
        src_ref=src,
        dst_ref=dst,
        send_sem=send_sem,
        recv_sem=recv_sem,
        device_id={"ctg": target},
        device_id_type=pl.DeviceIdType.MESH,
    )


def kernel(
    n, hour_rows, step_size, balance,
    tiles, pattern_hbm, index_hbm, table_hbm, base_hbm, dual_hbm, level_hbm, cost_hbm, ramp_hbm, demand_hbm,
    floor_hbm, span_hbm, ramp_limit_hbm, ramp_mask_hbm,
    out_levels, out_dual, out_ramp, out_price,
    masked, gates, pattern, pattern_rows, index, table, base_in, dual_in, unit_rows, mask_row, demand,
    dual, base, starts, limit, dual_half, flow_acc,
    start_stage, frag_in, frag_out,
    cost, levels, ramp, extended, halo_ext, halo_ramp,
    pull_out, pair_in, pull_sum, pull_in, ext_half, stats, flow_stat, price, omega,
    tile_sem, in_sem, out_sem, frag_send, frag_recv, fin_send, fin_recv,
    pair_send, pair_recv, pull_send, pull_recv, ext_send, ext_recv, pass_send, stat_send, stat_recv,
    core_sems, halo_sems,
):
    f32 = jnp.float32
    bf16 = jnp.bfloat16
    chips = n // 2
    members = ROWS // hour_rows
    groups = n // members
    chunks = chips // groups
    unit_count = tiles.shape[1]
    width = unit_count // chunks
    ctgs, lines = base_in.shape[1], base_in.shape[2]
    hours = groups * ROWS
    pairs = chunks // 2
    halves = lines // 128

    me = lax.axis_index("ctg")
    core = lax.rem(me, 2)
    chip = lax.div(me, 2)
    owner = core == 1
    partner = me + 1 - 2 * core
    my_chunk = lax.div(chip, groups)
    my_group = lax.rem(chip, groups)
    home_group = lax.div(me, members)
    home_row = lax.rem(me, members)
    my_pair = lax.div(my_chunk, 2)
    my_side = lax.rem(my_chunk, 2)
    my_rows = pl.ds(pl.multiple_of(my_group * ROWS, ROWS), ROWS)
    my_lanes = pl.ds(pl.multiple_of(my_chunk * width, 128), width)

    ahead = 1 - lax.div(my_pair, pairs // 2)

    def flip(place, length):
        return ahead * (length - 1 - place) + (1 - ahead) * place

    def skip(place, own, length):
        return place + lax.div(place + length - own, length)

    def far_pair(j):
        last = lax.div(j + 1, pairs)
        place = flip(skip(j, flip(my_pair, pairs), pairs), pairs)
        return last * my_pair + (1 - last) * place

    def near_pair(j):
        return far_pair(pairs - 1 - j)

    def far_chunk(j):
        second = lax.rem(j, 2)
        side = second * my_side + (1 - second) * (1 - my_side)
        return far_pair(lax.div(j, 2)) * 2 + side

    def sums_here(j):
        return ((j < chunks // 2) | (j == chunks - 1)) == owner

    def both_cores(c):
        gap = lax.div(c, 2) - my_pair
        return (gap <= REACH) & (gap >= -REACH)

    def block_rows(g):
        return pl.ds(pl.multiple_of(g * ROWS, ROWS), ROWS)

    def tile_copy(j):
        c = far_chunk(j)
        return pltpu.make_async_copy(
            tiles.at[:, pl.ds(pl.multiple_of(c * width, 128), width)], masked.at[c], tile_sem.at[j]
        )

    def staged(i):
        src, dst = (
            (pattern_hbm, pattern),
            (dual_hbm, dual_in),
            (demand_hbm, demand),
            (level_hbm, starts.at[0]),
            (cost_hbm, starts.at[1]),
            (ramp_hbm, starts.at[2]),
            (index_hbm, index),
            (table_hbm, table),
            (base_hbm, base_in),
            (floor_hbm.at[:, my_lanes], unit_rows.at[0]),
            (span_hbm.at[:, my_lanes], unit_rows.at[1]),
            (ramp_limit_hbm.at[:, my_lanes], unit_rows.at[2]),
            (ramp_mask_hbm.at[:, my_lanes], mask_row),
        )[i]
        return pltpu.make_async_copy(src, dst, in_sem.at[i])

    for i in range(2):
        staged(i).start()
    for j in range(IN_FLIGHT):
        tile_copy(j).start()

    barrier = pltpu.get_barrier_semaphore()

    @pl.loop(1, n)
    def _(d):
        pl.semaphore_signal(
            barrier, inc=1, device_id={"ctg": lax.rem(me + d, n)}, device_id_type=pl.DeviceIdType.MESH
        )

    for i in range(2, 13):
        staged(i).start()

    omega[...] = jnp.ones_like(omega)
    price[...] = jnp.zeros_like(price)

    tile_count = unit_count // 128
    tile_row = lax.broadcasted_iota(jnp.int32, (tile_count, unit_count), 0)
    tile_lane = lax.broadcasted_iota(jnp.int32, (tile_count, unit_count), 1)
    spread = jnp.where(lax.shift_right_logical(tile_lane, 7) == tile_row, 1.0, 0.0).astype(bf16)
    staged(0).wait()
    for k in range(ctgs):
        pattern_rows[k * halves:(k + 1) * halves, :] = pattern[k].astype(f32)
    gate_rows = jnp.dot(pattern_rows[...].astype(bf16), spread, preferred_element_type=f32)
    for c in range(chunks):
        gates[c] = gate_rows[:, c * width:(c + 1) * width]
    staged(1).wait()
    for k in range(ctgs):
        lanes = slice(k * lines, (k + 1) * lines)
        start_dual = dual_in[:, k, :]
        dual[:, lanes] = start_dual
        dual_half[:, lanes] = start_dual.astype(bf16)

    def frag_copy(c, target):
        return send(
            starts.at[:, :, pl.ds(pl.multiple_of(c * width, 128), width)],
            start_stage.at[home_row], frag_send.at[c], frag_recv.at[home_row], target,
        )

    def fin_copy(r, source_chunk, target):
        return send(
            frag_out.at[r], frag_in.at[source_chunk], fin_send.at[r], fin_recv.at[source_chunk], target
        )

    def stat_copy(slot, target_chip, sender_chip):
        return send(
            stats.at[slot, sender_chip], stats.at[slot, sender_chip],
            stat_send.at[slot % 2, target_chip], stat_recv.at[slot % 2, sender_chip], target_chip * 2 + 1,
        )

    def stat_start(slot):
        @pl.loop(1, chips)
        def _(d):
            stat_copy(slot, lax.rem(chip + d, chips), chip).start()

    def stat_wait(slot):
        @pl.loop(1, chips)
        def _(d):
            peer = lax.rem(chip + d, chips)
            stat_copy(slot, peer, chip).wait_send()
            stat_copy(slot, peer, peer).wait_recv()

    def flow_stat_copy(slot):
        return send(flow_stat.at[0], flow_stat.at[slot], core_sems.at[0], core_sems.at[1], partner)

    def omega_copy():
        return send(omega, omega, core_sems.at[2], core_sems.at[3], partner)

    def price_copy():
        return send(price, price, core_sems.at[4], core_sems.at[5], partner)

    def pair_copy(it, c):
        return send(pull_out.at[c], pair_in.at[it, c], pair_send.at[c], pair_recv.at[c], partner)

    def pull_copy(it, target_chip, sender_chip):
        c, g = lax.div(target_chip, groups), lax.rem(target_chip, groups)
        return send(
            pull_sum.at[c, block_rows(g)], pull_in.at[it, sender_chip],
            pull_send.at[target_chip], pull_recv.at[sender_chip], target_chip * 2 + 1,
        )

    def ext_copy(it, origin_chip, send_sem, target):
        c, g = lax.div(origin_chip, groups), lax.rem(origin_chip, groups)
        spot = ext_half.at[it, c, block_rows(g)]
        return send(spot, spot, send_sem, ext_recv.at[origin_chip], target)

    def ext_out(it, target):
        return ext_copy(it, chip, ext_send.at[target], target)

    def ext_pass(it, origin_chip):
        return ext_copy(it, origin_chip, pass_send.at[origin_chip], partner)

    def halo_ext_copy(it, target):
        return send(extended.at[pl.ds(0, 8)], halo_ext.at[it], halo_sems.at[0], halo_sems.at[1], target)

    def halo_ramp_copy(it, target):
        return send(ramp.at[pl.ds(ROWS - 8, 8)], halo_ramp.at[it], halo_sems.at[2], halo_sems.at[3], target)

    def product(c):
        pull_out[c] = jnp.dot(dual_half[...], masked[c], preferred_element_type=f32).astype(bf16)

    def pair_start(it, j):
        @pl.when(jnp.logical_not(sums_here(j)))
        def _():
            pair_copy(it, far_chunk(j)).start()

    def forward(it, j):
        @pl.when(sums_here(j))
        def _():
            c = far_chunk(j)
            pair_copy(it, c).wait_recv()
            for g in range(groups):
                rows = slice(g * ROWS, (g + 1) * ROWS)
                target_chip = c * groups + g
                both = (pull_out[c, rows, :].astype(f32) + pair_in[it, c, rows, :].astype(f32)).astype(bf16)

                @pl.when(target_chip != chip)
                def _():
                    pull_sum[c, rows, :] = both
                    pull_copy(it, target_chip, chip).start()

                @pl.when(target_chip == chip)
                def _():
                    pull_in[it, chip] = both

    def pull_sent(it):
        @pl.loop(0, chunks)
        def _(j):
            here = sums_here(j)
            c = far_chunk(j)

            @pl.when(jnp.logical_not(here))
            def _():
                pair_copy(it, c).wait_send()

            for g in range(groups):
                target_chip = c * groups + g

                @pl.when(here & (target_chip != chip))
                def _():
                    pull_copy(it, target_chip, chip).wait_send()

    def first_product(j):
        c = far_chunk(j)
        tile_copy(j).wait()

        @pl.when(j + IN_FLIGHT < chunks)
        def _():
            tile_copy(j + IN_FLIGHT).start()

        for r in range(ctgs * halves):
            gate = jnp.broadcast_to(gates[c, r:r + 1, :], (16, width)).astype(bf16)
            for q in range(8):
                where = slice(r * 128 + q * 16, r * 128 + q * 16 + 16)
                masked[c, where, :] = masked[c, where, :] * gate

        product(c)

    warm = chunks // 2

    @pl.loop(0, warm)
    def _(j):
        first_product(j)

    for i in range(2, 6):
        staged(i).wait()
    for r in range(hour_rows):
        starts[3, r:r + 1] = jnp.broadcast_to(demand[0:1, r:r + 1], (1, unit_count))
    pl.semaphore_wait(barrier, n - 1)

    @pl.loop(0, warm)
    def _(j):
        pair_start(0, j)

    for c in range(chunks):
        target = (c * groups + home_group) * 2 + 1

        @pl.when(target != me)
        def _():
            frag_copy(c, target).start()

        @pl.when(target == me)
        def _():
            start_stage[home_row] = starts[:, :, c * width:(c + 1) * width]

    @pl.loop(warm, chunks + warm)
    def _(j):
        @pl.when(j < chunks)
        def _():
            first_product(j)
            pair_start(0, j)

        forward(0, j - warm)

    for i in range(6, 13):
        staged(i).wait()

    row_iota = lax.broadcasted_iota(jnp.int32, (128, lines), 0)
    values = table[...].T
    part_a = values.astype(bf16)
    rest = values - part_a.astype(f32)
    part_b = rest.astype(bf16)
    part_c = (rest - part_b.astype(f32)).astype(bf16)
    for k in range(ctgs):
        which = index[k:k + 1, :]
        high = lax.shift_right_logical(which, 7)
        low = lax.bitwise_and(which, 127)
        blocks = table.shape[0] // 128
        got = jnp.zeros((128, lines), f32)
        for b in range(blocks):
            pick = jnp.where(row_iota + b * 128 == high, 1.0, 0.0).astype(bf16)
            for part in (part_a, part_b, part_c):
                got = got + jnp.dot(part[:, b * 128:(b + 1) * 128], pick, preferred_element_type=f32)
        limit[:, k * lines:(k + 1) * lines] = jnp.sum(
            jnp.where(row_iota == low, got, 0.0), axis=0, keepdims=True
        )
        base[:, k * lines:(k + 1) * lines] = base_in[:, k, :]

    block_row = lax.broadcasted_iota(jnp.int32, (ROWS, width), 0)
    lane_here = lax.broadcasted_iota(jnp.int32, (ROWS, 128), 1)
    row_here = lax.broadcasted_iota(jnp.int32, (ROWS, 128), 0) + my_group * ROWS
    diagonal = lane_here == row_here
    hour_lanes = lax.broadcasted_iota(jnp.int32, (1, 128), 1) < hours
    stat_row = lax.broadcasted_iota(jnp.int32, (4, 128), 0)

    def to_lanes(column):
        return jnp.sum(
            jnp.where(diagonal, jnp.broadcast_to(column, (ROWS, 128)), 0.0), axis=0, keepdims=True
        )

    def fold(x):
        rows, cols = x.shape
        out = None
        for r in range(0, rows, 8):
            for b in range(0, cols, 128):
                piece = x[r:r + 8, b:b + 128]
                out = piece if out is None else out + piece
        return jnp.sum(out, axis=0, keepdims=True)

    def halo_ramp_start(it):
        if groups > 1:
            @pl.when(my_group < groups - 1)
            def _():
                halo_ramp_copy(it, me + 2).start()

    @pl.when(owner)
    def _():
        for r in range(members):
            peer = my_group * members + r

            @pl.when(peer != me)
            def _():
                send(
                    starts.at[:, :, pl.ds(0, width)], start_stage.at[r],
                    frag_send.at[0], frag_recv.at[r], peer,
                ).wait_recv()

        demand_rows = []
        for r in range(members):
            rows = slice(r * hour_rows, (r + 1) * hour_rows)
            levels[rows, :] = start_stage[r, 0]
            cost[rows, :] = start_stage[r, 1]
            ramp[rows, :] = start_stage[r, 2]
            extended[rows, 0:128] = start_stage[r, 3, :, 0:128]
        lanes = to_lanes(extended[:, 0:1])
        mine = (stat_row == 0) & (jnp.full((4, 128), my_chunk) == 0)
        stats[0, chip] = jnp.where(mine, lanes, 0.0)
        stat_start(0)
        halo_ramp_start(0)

    for c in range(chunks):
        target = (c * groups + home_group) * 2 + 1

        @pl.when(target != me)
        def _():
            frag_copy(c, target).wait_send()

    def absorb(slot, sigma):
        total = stats[slot, 0]
        for q in range(1, chips):
            total = total + stats[slot, q]
        move = sigma * (balance * (total[0:1] - price[1:2]))
        move = jnp.where(hour_lanes, move, 0.0)
        price[0:1] = price[0:1] + move
        return total, jnp.sum(move * move, axis=1, keepdims=True)

    def primal(it):
        @pl.when(it > 0)
        def _():
            stat_wait(it)

        @pl.when(it == 1)
        def _():
            stat_wait(0)
            first = stats[0, 0]
            for q in range(1, chips):
                first = first + stats[0, q]
            price[1:2] = first[0:1]

        @pl.when(it > 0)
        def _():
            old = omega[0:1, 0:1]
            total, price_sq = absorb(it, step_size * old)
            sums = jnp.sum(total, axis=1, keepdims=True)
            dual_sq = sums[3:4] + sums[2:3] + price_sq
            ratio = (dual_sq + 1e-06) / (sums[1:2] + 1e-06)
            omega[...] = jnp.broadcast_to(jnp.sqrt(old) * jnp.sqrt(jnp.sqrt(ratio)), omega.shape)
            omega_copy().start()

        weight = omega[0:1, 0:1]
        tau = step_size / weight
        sigma = step_size * weight

        if groups > 1:
            @pl.when(my_group < groups - 1)
            def _():
                halo_ramp_copy(it, me + 2).wait_send()

            @pl.when(my_group > 0)
            def _():
                halo_ramp_copy(it, me - 2).wait_recv()

            @pl.when(my_group == 0)
            def _():
                halo_ramp[it] = jnp.zeros_like(halo_ramp[it])

            edge_ramp = halo_ramp[it][7:8]
        else:
            edge_ramp = jnp.zeros((1, width), f32)

        floor = unit_rows[0]
        ceiling = floor + unit_rows[1]
        ramp_limit = unit_rows[2]
        ramp_on = mask_row[...].astype(f32)
        ramp_now = ramp[...]
        before = jnp.where(block_row == 0, edge_ramp, pltpu.roll(ramp_now, 1, 0))
        price_here = jnp.sum(
            jnp.where(diagonal, jnp.broadcast_to(price[0:1], (ROWS, 128)), 0.0), axis=1, keepdims=True
        )
        known = cost[...] + ramp_on * (before - ramp_now) + balance * price_here

        @pl.loop(1, chips)
        def _(d):
            other = lax.rem(chip + d, chips)
            pull_copy(it, other, other).wait_recv()

        pulled = pull_in[it, 0].astype(f32)
        for q in range(1, chips):
            pulled = pulled + pull_in[it, q].astype(f32)

        gradient = known + pulled
        old_levels = levels[...]
        moved = jnp.clip(old_levels - tau * gradient, floor, ceiling)
        ext = 2.0 * moved - old_levels
        levels[...] = moved
        ext_half[it, my_chunk, my_rows, :] = ext.astype(bf16)
        extended[...] = ext

        @pl.loop(0, chunks)
        def _(j):
            c = far_chunk(j)
            for g in range(groups):
                other = c * groups + g

                @pl.when(other != chip)
                def _():
                    ext_out(it, other * 2 + 1).start()

                @pl.when(both_cores(c))
                def _():
                    ext_out(it, other * 2).start()

        if groups > 1:
            @pl.when(my_group > 0)
            def _():
                halo_ext_copy(it, me - 2).start()
                halo_ext_copy(it, me - 2).wait_send()

            @pl.when(my_group < groups - 1)
            def _():
                halo_ext_copy(it, me + 2).wait_recv()

            @pl.when(my_group == groups - 1)
            def _():
                halo_ext[it] = jnp.zeros_like(halo_ext[it])

            edge_ext = halo_ext[it][0:1]
        else:
            edge_ext = jnp.zeros((1, width), f32)

        after = jnp.where(block_row == ROWS - 1, edge_ext, pltpu.roll(ext, ROWS - 1, 0))
        change = ramp_on * (after - ext)
        last_hour = block_row + my_group * ROWS == hours - 1
        change = jnp.where(last_hour, 0.0, change)
        trial = ramp_now + sigma * change
        ramp_new = trial - sigma * jnp.clip(trial / sigma, -ramp_limit, ramp_limit)
        ramp[...] = ramp_new

        row_sums = to_lanes(jnp.sum(ext, axis=1, keepdims=True))
        primal_sq = fold((moved - old_levels) ** 2)
        ramp_sq = fold((ramp_new - ramp_now) ** 2)
        stats[it + 1, chip] = jnp.where(
            stat_row == 0, row_sums,
            jnp.where(stat_row == 1, primal_sq, jnp.where(stat_row == 2, ramp_sq, 0.0)),
        )

        @pl.when(it == ITERS - 1)
        def _():
            stat_start(it + 1)
            for r in range(members):
                rows = slice(r * hour_rows, (r + 1) * hour_rows)
                frag_out[r, 0] = moved[rows, :]
                frag_out[r, 1] = ramp_new[rows, :]
            for r in range(members):
                target = my_group * members + r

                @pl.when(target != me)
                def _():
                    fin_copy(r, my_chunk, target).start()

                @pl.when(target == me)
                def _():
                    frag_in[my_chunk] = frag_out[r]

    def take(it, c):
        for g in range(groups):
            other = c * groups + g

            @pl.when(jnp.logical_not(owner & (other == chip)))
            def _():
                ext_pass(it, other).wait_recv()

    def take_and_pass(it, c):
        take(it, c)

        @pl.when(owner & jnp.logical_not(both_cores(c)))
        def _():
            for g in range(groups):
                ext_pass(it, c * groups + g).start()

    def flow(x, w):
        return lax.dot_general(x, w, (((1,), (1,)), ((), ())), preferred_element_type=f32)

    @pl.loop(0, ITERS)
    def _(it):
        @pl.when(it > 0)
        def _():
            @pl.loop(0, chunks + LAG)
            def _(j):
                @pl.when(j < chunks)
                def _():
                    product(far_chunk(j))
                    pair_start(it, j)

                @pl.when((j == LAG) & owner)
                def _():
                    halo_ramp_start(it)
                    flow_stat_copy(it).wait_recv()
                    stats[it, chip, 3:4] = stats[it, chip, 3:4] + flow_stat[it, 0:1]
                    stat_start(it)

                @pl.when(j >= LAG)
                def _():
                    forward(it, j - LAG)

        pull_sent(it)

        @pl.when(owner)
        def _():
            primal(it)

        take(it, my_chunk)
        flow_acc[...] = flow(ext_half[it, my_chunk], masked[my_chunk])
        near = my_pair * 2 + 1 - my_side
        first = near_pair(1) * 2
        take_and_pass(it, first)
        take_and_pass(it, first + 1)
        take(it, near)
        flow_acc[...] += flow(ext_half[it, near], masked[near])

        @pl.loop(1, pairs)
        def _(j):
            @pl.when(j + 1 < pairs)
            def _():
                following = near_pair(j + 1) * 2
                take_and_pass(it, following)
                take_and_pass(it, following + 1)

            c = near_pair(j) * 2
            x = jnp.concatenate([ext_half[it, c], ext_half[it, c + 1]], axis=1)
            w = jnp.concatenate([masked[c], masked[c + 1]], axis=1)
            flow_acc[...] += flow(x, w)

        @pl.when(owner)
        def _():
            @pl.loop(0, chunks)
            def _(c):
                for g in range(groups):
                    other = c * groups + g

                    @pl.when(other != chip)
                    def _():
                        ext_out(it, other * 2 + 1).wait_send()

                    @pl.when(both_cores(c))
                    def _():
                        ext_out(it, other * 2).wait_send()

                    @pl.when(jnp.logical_not(both_cores(c)))
                    def _():
                        ext_pass(it, other).wait_send()

            @pl.when(it > 0)
            def _():
                omega_copy().wait_send()

        @pl.when((it > 0) & jnp.logical_not(owner))
        def _():
            omega_copy().wait_recv()

        sigma = step_size * omega[0:1, 0:1]
        old_dual = dual[...]
        trial = old_dual + sigma * flow_acc[...]
        bound = limit[...]
        dual_new = trial - sigma * jnp.clip(trial / sigma, base[...] - bound, base[...] + bound)
        dual[...] = dual_new
        dual_half[...] = dual_new.astype(bf16)

        @pl.when(it < ITERS - 1)
        def _():
            flow_sq = fold((dual_new - old_dual) ** 2)

            @pl.when(owner)
            def _():
                stats[it + 1, chip, 3:4] = flow_sq

            @pl.when(jnp.logical_not(owner))
            def _():
                @pl.when(it > 0)
                def _():
                    flow_stat_copy(it).wait_send()

                flow_stat[0] = jnp.broadcast_to(flow_sq, (8, 128))
                flow_stat_copy(it + 1).start()

    dual_out = pltpu.make_async_copy(dual, out_dual, out_sem.at[0])
    dual_out.start()

    @pl.when(owner)
    def _():
        stat_wait(ITERS)
        absorb(ITERS, step_size * omega[0:1, 0:1])
        price_copy().start()

    for c in range(chunks):
        peer = (c * groups + home_group) * 2 + 1

        @pl.when(peer != me)
        def _():
            fin_copy(0, c, peer).wait_recv()

    def level_out(c, which, out):
        return pltpu.make_async_copy(
            frag_in.at[c, which], out.at[:, pl.ds(c * width, width)], out_sem.at[2 + 2 * c + which]
        )

    for c in range(chunks):
        level_out(c, 0, out_levels).start()
        level_out(c, 1, out_ramp).start()

    @pl.when(owner)
    def _():
        for r in range(members):
            target = my_group * members + r

            @pl.when(target != me)
            def _():
                fin_copy(r, my_chunk, target).wait_send()

        price_copy().wait_send()

    @pl.when(jnp.logical_not(owner))
    def _():
        flow_stat_copy(0).wait_send()
        price_copy().wait_recv()

    price_out = pltpu.make_async_copy(price, out_price, out_sem.at[1])
    price_out.start()
    for c in range(chunks):
        level_out(c, 0, out_levels).wait()
        level_out(c, 1, out_ramp).wait()
    price_out.wait()
    dual_out.wait()


def finish(levels, dual, ramp, price, out_levels, out_dual, out_ramp, out_price):
    lines = out_dual.shape[2]
    out_levels[...] = levels[...]
    out_ramp[...] = ramp[...]
    for k in range(out_dual.shape[1]):
        out_dual[:, k, :] = dual[:, k * lines:(k + 1) * lines]
    hour_rows = out_price.shape[0]
    lane = lax.broadcasted_iota(jnp.int32, (1, 128), 1) - lax.axis_index("ctg") * hour_rows
    for r in range(hour_rows):
        out_price[r] = jnp.sum(jnp.where(lane == r, price[0:1], 0.0))


def body(
    flow_tiles,
    tile_pattern,
    monitored,
    ratings,
    base_flow,
    unit_cost,
    unit_floor,
    unit_span,
    ramp_limit,
    ramp_mask,
    demand,
    start_output,
    start_flow_dual,
    start_ramp_dual,
):
    f32, bf16 = jnp.float32, jnp.bfloat16
    ctgs, lines, unit_count = flow_tiles.shape
    n = lax.axis_size("ctg")
    hour_rows = start_output.shape[0]
    hours = hour_rows * n
    groups = hours // ROWS
    chips = n // 2
    chunks = chips // groups
    members = ROWS // hour_rows
    width = unit_count // chunks
    flat = ctgs * lines
    step_size = 0.5 / (2.0 + math.sqrt(ctgs * n * lines / unit_count))
    balance = 1.0 / math.sqrt(unit_count)

    gate_rows = ctgs * tile_pattern.shape[1]

    vmem = pl.BlockSpec(memory_space=pltpu.VMEM)
    hbm = pl.BlockSpec(memory_space=pl.ANY)
    sem = pltpu.SemaphoreType.DMA
    out = pl.pallas_call(
        functools.partial(kernel, n, hour_rows, step_size, balance),
        out_shape=(
            jax.ShapeDtypeStruct((hour_rows, unit_count), f32),
            jax.ShapeDtypeStruct((hours, flat), f32),
            jax.ShapeDtypeStruct((hour_rows, unit_count), f32),
            jax.ShapeDtypeStruct((8, 128), f32),
        ),
        in_specs=[hbm] * 14,
        out_specs=(hbm,) * 4,
        scratch_shapes=[
            pltpu.VMEM((chunks, flat, width), bf16),
            pltpu.VMEM((chunks, gate_rows, width), f32),
            pltpu.VMEM(tile_pattern.shape, jnp.int32),
            pltpu.VMEM((gate_rows, tile_pattern.shape[2]), f32),
            pltpu.VMEM(monitored.shape, jnp.int32),
            pltpu.VMEM((ratings.shape[0] // 128, 128), f32),
            pltpu.VMEM(base_flow.shape, f32),
            pltpu.VMEM(start_flow_dual.shape, f32),
            pltpu.VMEM((3, 1, width), f32),
            pltpu.VMEM((1, width), jnp.int32),
            pltpu.VMEM((1, hour_rows), f32),
            pltpu.VMEM((hours, flat), f32),
            pltpu.VMEM((hours, flat), f32),
            pltpu.VMEM((4, hour_rows, unit_count), f32),
            pltpu.VMEM((1, flat), f32),
            pltpu.VMEM((hours, flat), bf16),
            pltpu.VMEM((hours, flat), f32),
            pltpu.VMEM((members, 4, hour_rows, width), f32),
            pltpu.VMEM((chunks, 2, hour_rows, width), f32),
            pltpu.VMEM((members, 2, hour_rows, width), f32),
            pltpu.VMEM((ROWS, width), f32),
            pltpu.VMEM((ROWS, width), f32),
            pltpu.VMEM((ROWS, width), f32),
            pltpu.VMEM((ROWS, width), f32),
            pltpu.VMEM((ITERS, 8, width), f32),
            pltpu.VMEM((ITERS, 8, width), f32),
            pltpu.VMEM((chunks, hours, width), bf16),
            pltpu.VMEM((ITERS, chunks, hours, width), bf16),
            pltpu.VMEM((chunks, hours, width), bf16),
            pltpu.VMEM((ITERS, chips, ROWS, width), bf16),
            pltpu.VMEM((ITERS, chunks, hours, width), bf16),
            pltpu.VMEM((ITERS + 1, chips, 4, 128), f32),
            pltpu.VMEM((ITERS, 8, 128), f32),
            pltpu.VMEM((8, 128), f32),
            pltpu.VMEM((8, 128), f32),
            sem((chunks,)), sem((13,)), sem((2 + 2 * chunks,)),
            sem((chunks,)), sem((members,)), sem((members,)), sem((chunks,)),
            sem((chunks,)), sem((chunks,)), sem((chips,)), sem((chips,)),
            sem((n,)), sem((chips,)), sem((chips,)),
            sem((2, chips)), sem((2, chips)),
            sem((6,)), sem((4,)),
        ],
        compiler_params=pltpu.CompilerParams(collective_id=0, has_side_effects=True),
    )(
        flow_tiles.reshape(flat, unit_count),
        tile_pattern,
        monitored,
        ratings.reshape(-1, 128),
        base_flow,
        start_flow_dual,
        start_output,
        unit_cost,
        start_ramp_dual,
        demand[None],
        unit_floor[None],
        unit_span[None],
        ramp_limit[None],
        ramp_mask[None],
    )
    return pl.pallas_call(
        finish,
        out_shape=(
            jax.ShapeDtypeStruct((hour_rows, unit_count), f32),
            jax.ShapeDtypeStruct((hours, ctgs, lines), f32),
            jax.ShapeDtypeStruct((hour_rows, unit_count), f32),
            jax.ShapeDtypeStruct((hour_rows,), f32),
        ),
        in_specs=[vmem] * 4,
        out_specs=(vmem,) * 3 + (pl.BlockSpec(memory_space=pltpu.SMEM),),
    )(*out)


def solution(mesh):
    return jax.shard_map(
        body,
        mesh=mesh,
        in_specs=(
            P("ctg", None, None),
            P("ctg", None, None),
            P("ctg", None),
            P(),
            P("grp", "ctg", None),
            P(("grp", "ctg"), None),
            P(),
            P(),
            P(),
            P(),
            P(("grp", "ctg")),
            P(("grp", "ctg"), None),
            P("grp", "ctg", None),
            P(("grp", "ctg"), None),
        ),
        out_specs=(
            P(("grp", "ctg"), None),
            P("grp", "ctg", None),
            P(("grp", "ctg"), None),
            P(("grp", "ctg")),
        ),
        check_vma=False,
    )
```

time: 78.3 us -> 72.2 us (0.922)
  Pallas kernels: 77.5 us -> 71.4 us
    pallas_call x1, Pallas kernels: 75.7 us -> 69.7 us  [body(): pl.pallas_call(functools.partial(kernel, n, hour_rows, step_size, balance...]
where the time goes in v1:
time: 72.2 us; the launch traced here: 72.1 us
  Pallas kernels  71.4 us (99%)
    pallas_call x1, Pallas kernels, body(): pl.pallas_call(functools.partial(kernel, n, hour_rows, step_size, balance...  69.7 us
    pallas_call x1, Pallas kernels, body(): pl.pallas_call(finish, out_shape=(jax.ShapeDtypeStruct((hour_rows, unit_c...  1.76 us

profile of v1, /device:TPU:0, one launch (start us, length us, event | category | flops | bytes accessed | tf_op | source)
XLA Modules:
  0.0 72.1 jit_solution(2021947903958822595)
XLA Ops:
  0.6 69.7 %shard_map.165 = (f32[2,3072]{1,0:T(2,128)}, f32[32,2048]{1,0:T(8,128)}, f32[2,3072]{1,0:T(2,128)}, f32[8,128]{1,0:T(8,128)}) custom-call(bf16[2048,3072]{1,0:T(8,128)(2,1)} %bitcast.7, s32[8,2,24]{2,1,0:T(2,128)} %pattern_hbm.1, s32[8,256]{1,0:T(8,128)} %index_hbm.1, f32[128,128]{1,0:T(8,128)} %bitcast.8, f32[32,8,256]{2,1,0:T(8,128)} %base_hbm.1, ...), custom_call_target="tpu_custom_call" | custom-call | tf_op jit(solution)/shard_map/pallas_call | solution.py:770
  70.3 1.8 %shard_map.166 = (f32[2,3072]{1,0:T(2,128)}, f32[32,8,256]{2,1,0:T(8,128)}, f32[2,3072]{1,0:T(2,128)}, f32[2]{0:T(128)}) custom-call(f32[2,3072]{1,0:T(2,128)} %get-tuple-element.8.levels, f32[32,2048]{1,0:T(8,128)} %get-tuple-element.9.dual, f32[2,3072]{1,0:T(2,128)} %get-tuple-element.10.ramp, f32[8,128]{1,0:T(8,128)} %get-tuple-element.11.price), custom_call_target="tpu_custom_call" | custom-call | tf_op jit(solution)/shard_map/pallas_call | solution.py:840

commit v2 on v1

--- a/solution.py
+++ b/solution.py
@@ -10,9 +10,10 @@
 
 ITERS = 4
 ROWS = 32
-LAG = 3
+STAT = 3
+LAG = 0
+AHEAD = 1
 IN_FLIGHT = 3
-REACH = 1
 
 
 def send(src, dst, send_sem, recv_sem, target):
@@ -31,13 +32,12 @@
     tiles, pattern_hbm, index_hbm, table_hbm, base_hbm, dual_hbm, level_hbm, cost_hbm, ramp_hbm, demand_hbm,
     floor_hbm, span_hbm, ramp_limit_hbm, ramp_mask_hbm,
     out_levels, out_dual, out_ramp, out_price,
-    masked, gates, pattern, pattern_rows, index, table, base_in, dual_in, unit_rows, mask_row, demand,
+    masked, turned, gates, pattern, pattern_rows, index, table, base_in, dual_in, unit_rows, mask_row, demand,
     dual, base, starts, limit, dual_half, flow_acc,
     start_stage, frag_in, frag_out,
     cost, levels, ramp, extended, halo_ext, halo_ramp,
     pull_out, pair_in, pull_sum, pull_in, ext_half, stats, flow_stat, price, omega,
-    tile_sem, in_sem, out_sem, frag_send, frag_recv, fin_send, fin_recv,
-    pair_send, pair_recv, pull_send, pull_recv, ext_send, ext_recv, pass_send, stat_send, stat_recv,
+    frag_send, frag_recv, pair_recv, pull_send, pull_recv, ext_send, ext_recv, stat_send, stat_recv,
     core_sems, halo_sems,
 ):
     f32 = jnp.float32
@@ -89,11 +89,10 @@
         return far_pair(lax.div(j, 2)) * 2 + side
 
     def sums_here(j):
-        return ((j < chunks // 2) | (j == chunks - 1)) == owner
+        return (j >= EARLY) == owner
 
     def both_cores(c):
-        gap = lax.div(c, 2) - my_pair
-        return (gap <= REACH) & (gap >= -REACH)
+        return lax.div(c, 2) == my_pair
 
     def block_rows(g):
         return pl.ds(pl.multiple_of(g * ROWS, ROWS), ROWS)
@@ -101,7 +100,7 @@
     def tile_copy(j):
         c = far_chunk(j)
         return pltpu.make_async_copy(
-            tiles.at[:, pl.ds(pl.multiple_of(c * width, 128), width)], masked.at[c], tile_sem.at[j]
+            tiles.at[:, pl.ds(pl.multiple_of(c * width, 128), width)], masked.at[c], stat_send.at[j]
         )
 
     def staged(i):
@@ -120,12 +119,11 @@
             (ramp_limit_hbm.at[:, my_lanes], unit_rows.at[2]),
             (ramp_mask_hbm.at[:, my_lanes], mask_row),
         )[i]
-        return pltpu.make_async_copy(src, dst, in_sem.at[i])
+        return pltpu.make_async_copy(src, dst, core_sems.at[i - 3] if i in (6, 7, 8) else ext_send.at[i])
 
     for i in range(2):
         staged(i).start()
-    for j in range(IN_FLIGHT):
-        tile_copy(j).start()
+    tile_copy(0).start()
 
     barrier = pltpu.get_barrier_semaphore()
 
@@ -135,28 +133,22 @@
             barrier, inc=1, device_id={"ctg": lax.rem(me + d, n)}, device_id_type=pl.DeviceIdType.MESH
         )
 
+    for j in range(1, IN_FLIGHT):
+        tile_copy(j).start()
     for i in range(2, 13):
         staged(i).start()
 
     omega[...] = jnp.ones_like(omega)
     price[...] = jnp.zeros_like(price)
 
-    tile_count = unit_count // 128
-    tile_row = lax.broadcasted_iota(jnp.int32, (tile_count, unit_count), 0)
-    tile_lane = lax.broadcasted_iota(jnp.int32, (tile_count, unit_count), 1)
-    spread = jnp.where(lax.shift_right_logical(tile_lane, 7) == tile_row, 1.0, 0.0).astype(bf16)
     staged(0).wait()
     for k in range(ctgs):
         pattern_rows[k * halves:(k + 1) * halves, :] = pattern[k].astype(f32)
-    gate_rows = jnp.dot(pattern_rows[...].astype(bf16), spread, preferred_element_type=f32)
-    for c in range(chunks):
-        gates[c] = gate_rows[:, c * width:(c + 1) * width]
-    staged(1).wait()
-    for k in range(ctgs):
-        lanes = slice(k * lines, (k + 1) * lines)
-        start_dual = dual_in[:, k, :]
-        dual[:, lanes] = start_dual
-        dual_half[:, lanes] = start_dual.astype(bf16)
+    for b in range(unit_count // 128):
+        place = b * 128 % width
+        gates[b * 128 // width, :, place:place + 128] = jnp.broadcast_to(
+            pattern_rows[:, b:b + 1], (ctgs * halves, 128)
+        )
 
     def frag_copy(c, target):
         return send(
@@ -166,13 +158,13 @@
 
     def fin_copy(r, source_chunk, target):
         return send(
-            frag_out.at[r], frag_in.at[source_chunk], fin_send.at[r], fin_recv.at[source_chunk], target
+            frag_out.at[r], frag_in.at[source_chunk], frag_recv.at[r], frag_send.at[source_chunk], target
         )
 
     def stat_copy(slot, target_chip, sender_chip):
         return send(
             stats.at[slot, sender_chip], stats.at[slot, sender_chip],
-            stat_send.at[slot % 2, target_chip], stat_recv.at[slot % 2, sender_chip], target_chip * 2 + 1,
+            stat_send.at[target_chip], stat_recv.at[slot % 2, sender_chip], target_chip * 2 + 1,
         )
 
     def stat_start(slot):
@@ -197,13 +189,13 @@
         return send(price, price, core_sems.at[4], core_sems.at[5], partner)
 
     def pair_copy(it, c):
-        return send(pull_out.at[c], pair_in.at[it, c], pair_send.at[c], pair_recv.at[c], partner)
-
-    def pull_copy(it, target_chip, sender_chip):
+        return send(pull_out.at[c], pair_in.at[it, c], pull_send.at[c * groups], pair_recv.at[c], partner)
+
+    def pull_copy(it, src, target_chip, sender):
         c, g = lax.div(target_chip, groups), lax.rem(target_chip, groups)
         return send(
-            pull_sum.at[c, block_rows(g)], pull_in.at[it, sender_chip],
-            pull_send.at[target_chip], pull_recv.at[sender_chip], target_chip * 2 + 1,
+            src.at[c, block_rows(g)], pull_in.at[it, sender],
+            pull_send.at[target_chip], pull_recv.at[sender], target_chip * 2 + 1,
         )
 
     def ext_copy(it, origin_chip, send_sem, target):
@@ -215,7 +207,7 @@
         return ext_copy(it, chip, ext_send.at[target], target)
 
     def ext_pass(it, origin_chip):
-        return ext_copy(it, origin_chip, pass_send.at[origin_chip], partner)
+        return ext_copy(it, origin_chip, ext_send.at[origin_chip * 2], partner)
 
     def halo_ext_copy(it, target):
         return send(extended.at[pl.ds(0, 8)], halo_ext.at[it], halo_sems.at[0], halo_sems.at[1], target)
@@ -226,48 +218,55 @@
     def product(c):
         pull_out[c] = jnp.dot(dual_half[...], masked[c], preferred_element_type=f32).astype(bf16)
 
-    def pair_start(it, j):
-        @pl.when(jnp.logical_not(sums_here(j)))
-        def _():
-            pair_copy(it, far_chunk(j)).start()
+    def deliver(it, j):
+        c = far_chunk(j)
+
+        @pl.when((j < chunks // 2) & owner)
+        def _():
+            pair_copy(it, c).start()
+
+        @pl.when(j >= chunks // 2)
+        def _():
+            for g in range(groups):
+                target_chip = c * groups + g
+                here = owner & (target_chip == chip)
+
+                @pl.when(here)
+                def _():
+                    pull_in[it, me] = pull_out[c, g * ROWS:(g + 1) * ROWS, :]
+
+                @pl.when(jnp.logical_not(here))
+                def _():
+                    pull_copy(it, pull_out, target_chip, me).start()
 
     def forward(it, j):
-        @pl.when(sums_here(j))
+        @pl.when((j >= 0) & (j < chunks // 2) & jnp.logical_not(owner))
         def _():
             c = far_chunk(j)
             pair_copy(it, c).wait_recv()
+            pull_sum[c] = (pull_out[c].astype(f32) + pair_in[it, c].astype(f32)).astype(bf16)
             for g in range(groups):
-                rows = slice(g * ROWS, (g + 1) * ROWS)
-                target_chip = c * groups + g
-                both = (pull_out[c, rows, :].astype(f32) + pair_in[it, c, rows, :].astype(f32)).astype(bf16)
-
-                @pl.when(target_chip != chip)
-                def _():
-                    pull_sum[c, rows, :] = both
-                    pull_copy(it, target_chip, chip).start()
-
-                @pl.when(target_chip == chip)
-                def _():
-                    pull_in[it, chip] = both
+                pull_copy(it, pull_sum, c * groups + g, me).start()
 
     def pull_sent(it):
         @pl.loop(0, chunks)
         def _(j):
-            here = sums_here(j)
             c = far_chunk(j)
-
-            @pl.when(jnp.logical_not(here))
+            paired = (j < chunks // 2) & owner
+
+            @pl.when(paired)
             def _():
                 pair_copy(it, c).wait_send()
 
             for g in range(groups):
                 target_chip = c * groups + g
-
-                @pl.when(here & (target_chip != chip))
-                def _():
-                    pull_copy(it, target_chip, chip).wait_send()
-
-    def first_product(j):
+                here = owner & (target_chip == chip)
+
+                @pl.when(jnp.logical_not(paired | here))
+                def _():
+                    pull_copy(it, pull_out, target_chip, me).wait_send()
+
+    def mask(j):
         c = far_chunk(j)
         tile_copy(j).wait()
 
@@ -281,67 +280,53 @@
                 where = slice(r * 128 + q * 16, r * 128 + q * 16 + 16)
                 masked[c, where, :] = masked[c, where, :] * gate
 
-        product(c)
-
-    warm = chunks // 2
-
-    @pl.loop(0, warm)
-    def _(j):
-        first_product(j)
-
-    for i in range(2, 6):
-        staged(i).wait()
-    for r in range(hour_rows):
-        starts[3, r:r + 1] = jnp.broadcast_to(demand[0:1, r:r + 1], (1, unit_count))
-    pl.semaphore_wait(barrier, n - 1)
-
-    @pl.loop(0, warm)
-    def _(j):
-        pair_start(0, j)
-
-    for c in range(chunks):
-        target = (c * groups + home_group) * 2 + 1
-
-        @pl.when(target != me)
-        def _():
-            frag_copy(c, target).start()
-
-        @pl.when(target == me)
-        def _():
-            start_stage[home_row] = starts[:, :, c * width:(c + 1) * width]
-
-    @pl.loop(warm, chunks + warm)
+    first_lag = 2
+
+    @pl.loop(0, chunks + first_lag)
     def _(j):
         @pl.when(j < chunks)
         def _():
-            first_product(j)
-            pair_start(0, j)
-
-        forward(0, j - warm)
-
-    for i in range(6, 13):
+            mask(j)
+
+        @pl.when(j == 0)
+        def _():
+            staged(1).wait()
+            for k in range(ctgs):
+                lanes = slice(k * lines, (k + 1) * lines)
+                start_dual = dual_in[:, k, :]
+                dual[:, lanes] = start_dual
+                dual_half[:, lanes] = start_dual.astype(bf16)
+
+        @pl.when(j < chunks)
+        def _():
+            product(far_chunk(j))
+
+        @pl.when(j == 0)
+        def _():
+            for i in range(2, 6):
+                staged(i).wait()
+            for r in range(hour_rows):
+                starts[3, r:r + 1] = jnp.broadcast_to(demand[0:1, r:r + 1], (1, unit_count))
+            pl.semaphore_wait(barrier, n - 1)
+            for c in range(chunks):
+                target = (c * groups + home_group) * 2 + 1
+
+                @pl.when(target != me)
+                def _():
+                    frag_copy(c, target).start()
+
+                @pl.when(target == me)
+                def _():
+                    start_stage[home_row] = starts[:, :, c * width:(c + 1) * width]
+
+        @pl.when(j < chunks)
+        def _():
+            deliver(0, j)
+
+        forward(0, j - first_lag)
+
+    for i in range(9, 13):
         staged(i).wait()
-
-    row_iota = lax.broadcasted_iota(jnp.int32, (128, lines), 0)
-    values = table[...].T
-    part_a = values.astype(bf16)
-    rest = values - part_a.astype(f32)
-    part_b = rest.astype(bf16)
-    part_c = (rest - part_b.astype(f32)).astype(bf16)
-    for k in range(ctgs):
-        which = index[k:k + 1, :]
-        high = lax.shift_right_logical(which, 7)
-        low = lax.bitwise_and(which, 127)
-        blocks = table.shape[0] // 128
-        got = jnp.zeros((128, lines), f32)
-        for b in range(blocks):
-            pick = jnp.where(row_iota + b * 128 == high, 1.0, 0.0).astype(bf16)
-            for part in (part_a, part_b, part_c):
-                got = got + jnp.dot(part[:, b * 128:(b + 1) * 128], pick, preferred_element_type=f32)
-        limit[:, k * lines:(k + 1) * lines] = jnp.sum(
-            jnp.where(row_iota == low, got, 0.0), axis=0, keepdims=True
-        )
-        base[:, k * lines:(k + 1) * lines] = base_in[:, k, :]
 
     block_row = lax.broadcasted_iota(jnp.int32, (ROWS, width), 0)
     lane_here = lax.broadcasted_iota(jnp.int32, (ROWS, 128), 1)
@@ -416,14 +401,6 @@
         def _():
             stat_wait(it)
 
-        @pl.when(it == 1)
-        def _():
-            stat_wait(0)
-            first = stats[0, 0]
-            for q in range(1, chips):
-                first = first + stats[0, q]
-            price[1:2] = first[0:1]
-
         @pl.when(it > 0)
         def _():
             old = omega[0:1, 0:1]
@@ -466,14 +443,23 @@
         )
         known = cost[...] + ramp_on * (before - ramp_now) + balance * price_here
 
-        @pl.loop(1, chips)
-        def _(d):
-            other = lax.rem(chip + d, chips)
-            pull_copy(it, other, other).wait_recv()
+        first_near = lax.div(my_pair, pairs // 2) * (chips // 2)
+
+        @pl.loop(0, chips)
+        def _(q):
+            pull_copy(it, pull_out, q, q * 2).wait_recv()
+
+        @pl.loop(0, chips // 2)
+        def _(q):
+            @pl.when(first_near + q != chip)
+            def _():
+                pull_copy(it, pull_out, q, (first_near + q) * 2 + 1).wait_recv()
 
         pulled = pull_in[it, 0].astype(f32)
         for q in range(1, chips):
-            pulled = pulled + pull_in[it, q].astype(f32)
+            pulled = pulled + pull_in[it, q * 2].astype(f32)
+        for q in range(chips // 2):
+            pulled = pulled + pull_in[it, (first_near + q) * 2 + 1].astype(f32)
 
         gradient = known + pulled
         old_levels = levels[...]
@@ -520,7 +506,7 @@
         last_hour = block_row + my_group * ROWS == hours - 1
         change = jnp.where(last_hour, 0.0, change)
         trial = ramp_now + sigma * change
-        ramp_new = trial - sigma * jnp.clip(trial / sigma, -ramp_limit, ramp_limit)
+        ramp_new = trial - jnp.clip(trial, -sigma * ramp_limit, sigma * ramp_limit)
         ramp[...] = ramp_new
 
         row_sums = to_lanes(jnp.sum(ext, axis=1, keepdims=True))
@@ -549,6 +535,31 @@
                 def _():
                     frag_in[my_chunk] = frag_out[r]
 
+    def line_limits():
+        for i in range(6, 9):
+            staged(i).wait()
+
+        row_iota = lax.broadcasted_iota(jnp.int32, (128, lines), 0)
+        values = table[...].T
+        part_a = values.astype(bf16)
+        rest = values - part_a.astype(f32)
+        part_b = rest.astype(bf16)
+        part_c = (rest - part_b.astype(f32)).astype(bf16)
+        for k in range(ctgs):
+            which = index[k:k + 1, :]
+            high = lax.shift_right_logical(which, 7)
+            low = lax.bitwise_and(which, 127)
+            blocks = table.shape[0] // 128
+            got = jnp.zeros((128, lines), f32)
+            for b in range(blocks):
+                pick = jnp.where(row_iota + b * 128 == high, 1.0, 0.0).astype(bf16)
+                for part in (part_a, part_b, part_c):
+                    got = got + jnp.dot(part[:, b * 128:(b + 1) * 128], pick, preferred_element_type=f32)
+            limit[:, k * lines:(k + 1) * lines] = jnp.sum(
+                jnp.where(row_iota == low, got, 0.0), axis=0, keepdims=True
+            )
+            base[:, k * lines:(k + 1) * lines] = base_in[:, k, :]
+
     def take(it, c):
         for g in range(groups):
             other = c * groups + g
@@ -568,27 +579,57 @@
     def flow(x, w):
         return lax.dot_general(x, w, (((1,), (1,)), ((), ())), preferred_element_type=f32)
 
+    def small_out(i):
+        src, dst = ((price, out_price), (starts.at[0], out_levels), (starts.at[1], out_ramp))[i]
+        return pltpu.make_async_copy(src, dst, pull_recv.at[i])
+
+    def write_small():
+        @pl.when(owner)
+        def _():
+            stat_wait(ITERS)
+            absorb(ITERS, step_size * omega[0:1, 0:1])
+            price_copy().start()
+
+        for c in range(chunks):
+            peer = (c * groups + home_group) * 2 + 1
+
+            @pl.when(peer != me)
+            def _():
+                fin_copy(0, c, peer).wait_recv()
+
+        for c in range(chunks):
+            for which in range(2):
+                starts[which, :, c * width:(c + 1) * width] = frag_in[c, which]
+        small_out(1).start()
+        small_out(2).start()
+
     @pl.loop(0, ITERS)
     def _(it):
         @pl.when(it > 0)
         def _():
-            @pl.loop(0, chunks + LAG)
+            @pl.loop(0, chunks)
             def _(j):
-                @pl.when(j < chunks)
-                def _():
-                    product(far_chunk(j))
-                    pair_start(it, j)
-
-                @pl.when((j == LAG) & owner)
+                product(far_chunk(j))
+                deliver(it, j)
+
+                @pl.when((j == STAT) & owner)
                 def _():
                     halo_ramp_start(it)
                     flow_stat_copy(it).wait_recv()
                     stats[it, chip, 3:4] = stats[it, chip, 3:4] + flow_stat[it, 0:1]
                     stat_start(it)
 
-                @pl.when(j >= LAG)
-                def _():
-                    forward(it, j - LAG)
+                forward(it, j - LAG)
+
+            turn = (chunks - 1) // 2
+
+            @pl.when(it < 3)
+            def _():
+                @pl.loop(0, turn * (ctgs * lines // 256))
+                def _(i):
+                    j = (it - 1) * turn + lax.div(i, ctgs * lines // 256)
+                    block = pl.ds(pl.multiple_of(lax.rem(i, ctgs * lines // 256) * 256, 256), 256)
+                    turned[j, :, block] = masked[far_chunk(j), block, :].T
 
         pull_sent(it)
 
@@ -598,25 +639,43 @@
 
         take(it, my_chunk)
         flow_acc[...] = flow(ext_half[it, my_chunk], masked[my_chunk])
+
+        @pl.when(it == 0)
+        def _():
+            line_limits()
+
         near = my_pair * 2 + 1 - my_side
-        first = near_pair(1) * 2
-        take_and_pass(it, first)
-        take_and_pass(it, first + 1)
         take(it, near)
         flow_acc[...] += flow(ext_half[it, near], masked[near])
 
-        @pl.loop(1, pairs)
+        @pl.loop(1, pairs + AHEAD)
         def _(j):
-            @pl.when(j + 1 < pairs)
-            def _():
-                following = near_pair(j + 1) * 2
-                take_and_pass(it, following)
-                take_and_pass(it, following + 1)
-
-            c = near_pair(j) * 2
-            x = jnp.concatenate([ext_half[it, c], ext_half[it, c + 1]], axis=1)
-            w = jnp.concatenate([masked[c], masked[c + 1]], axis=1)
-            flow_acc[...] += flow(x, w)
+            @pl.when(j < pairs)
+            def _():
+                c = near_pair(j) * 2
+                take_and_pass(it, c)
+                take_and_pass(it, c + 1)
+
+            @pl.when((it == ITERS - 1) & (j == pairs))
+            def _():
+                write_small()
+
+            @pl.when(j > AHEAD)
+            def _():
+                place = (pairs - 1 - j + AHEAD) * 2
+                c, d = far_chunk(place), far_chunk(place + 1)
+                x = jnp.concatenate([ext_half[it, c], ext_half[it, d]], axis=1)
+                ready = (it > 1) | ((it == 1) & (place + 1 < (chunks - 1) // 2))
+
+                @pl.when(ready)
+                def _():
+                    w = jnp.concatenate([turned[place], turned[place + 1]], axis=0)
+                    flow_acc[...] += jnp.dot(x, w, preferred_element_type=f32)
+
+                @pl.when(jnp.logical_not(ready))
+                def _():
+                    w = jnp.concatenate([masked[c], masked[d]], axis=1)
+                    flow_acc[...] += flow(x, w)
 
         @pl.when(owner)
         def _():
@@ -641,15 +700,31 @@
             def _():
                 omega_copy().wait_send()
 
+        @pl.when((it == 0) & owner)
+        def _():
+            stat_wait(0)
+            first = stats[0, 0]
+            for q in range(1, chips):
+                first = first + stats[0, q]
+            price[1:2] = first[0:1]
+
         @pl.when((it > 0) & jnp.logical_not(owner))
         def _():
             omega_copy().wait_recv()
+
+        @pl.when(it == ITERS - 1)
+        def _():
+            @pl.when(jnp.logical_not(owner))
+            def _():
+                price_copy().wait_recv()
+
+            small_out(0).start()
 
         sigma = step_size * omega[0:1, 0:1]
         old_dual = dual[...]
         trial = old_dual + sigma * flow_acc[...]
         bound = limit[...]
-        dual_new = trial - sigma * jnp.clip(trial / sigma, base[...] - bound, base[...] + bound)
+        dual_new = trial - jnp.clip(trial, sigma * (base[...] - bound), sigma * (base[...] + bound))
         dual[...] = dual_new
         dual_half[...] = dual_new.astype(bf16)
 
@@ -670,30 +745,8 @@
                 flow_stat[0] = jnp.broadcast_to(flow_sq, (8, 128))
                 flow_stat_copy(it + 1).start()
 
-    dual_out = pltpu.make_async_copy(dual, out_dual, out_sem.at[0])
+    dual_out = pltpu.make_async_copy(dual, out_dual, ext_send.at[0])
     dual_out.start()
-
-    @pl.when(owner)
-    def _():
-        stat_wait(ITERS)
-        absorb(ITERS, step_size * omega[0:1, 0:1])
-        price_copy().start()
-
-    for c in range(chunks):
-        peer = (c * groups + home_group) * 2 + 1
-
-        @pl.when(peer != me)
-        def _():
-            fin_copy(0, c, peer).wait_recv()
-
-    def level_out(c, which, out):
-        return pltpu.make_async_copy(
-            frag_in.at[c, which], out.at[:, pl.ds(c * width, width)], out_sem.at[2 + 2 * c + which]
-        )
-
-    for c in range(chunks):
-        level_out(c, 0, out_levels).start()
-        level_out(c, 1, out_ramp).start()
 
     @pl.when(owner)
     def _():
@@ -709,27 +762,59 @@
     @pl.when(jnp.logical_not(owner))
     def _():
         flow_stat_copy(0).wait_send()
-        price_copy().wait_recv()
-
-    price_out = pltpu.make_async_copy(price, out_price, out_sem.at[1])
-    price_out.start()
-    for c in range(chunks):
-        level_out(c, 0, out_levels).wait()
-        level_out(c, 1, out_ramp).wait()
-    price_out.wait()
+
+    for i in range(3):
+        small_out(i).wait()
     dual_out.wait()
 
 
-def finish(levels, dual, ramp, price, out_levels, out_dual, out_ramp, out_price):
-    lines = out_dual.shape[2]
-    out_levels[...] = levels[...]
-    out_ramp[...] = ramp[...]
-    for k in range(out_dual.shape[1]):
-        out_dual[:, k, :] = dual[:, k * lines:(k + 1) * lines]
-    hour_rows = out_price.shape[0]
+def finish(
+    levels, dual, ramp, price, out_levels, out_dual, out_ramp, out_price,
+    level_box, dual_box, tile_box, ramp_box, price_box, own_price, in_sem, out_sem,
+):
+    hours, ctgs, lines = out_dual.shape
+    hour_rows = own_price.shape[1]
+    pieces = hours // 8
+
+    def dual_in(p):
+        return pltpu.make_async_copy(dual.at[p * 8:p * 8 + 8], dual_box.at[p], in_sem.at[3 + p])
+
+    def dual_out(p):
+        return pltpu.make_async_copy(tile_box.at[p], out_dual.at[p * 8:p * 8 + 8], out_sem.at[3 + p])
+
+    small_in = (
+        pltpu.make_async_copy(price, price_box, in_sem.at[0]),
+        pltpu.make_async_copy(levels, level_box, in_sem.at[1]),
+        pltpu.make_async_copy(ramp, ramp_box, in_sem.at[2]),
+    )
+    small_out = (
+        pltpu.make_async_copy(own_price, out_price, out_sem.at[0]),
+        pltpu.make_async_copy(level_box, out_levels, out_sem.at[1]),
+        pltpu.make_async_copy(ramp_box, out_ramp, out_sem.at[2]),
+    )
+    for p in range(pieces):
+        dual_in(p).start()
+    for copy in small_in:
+        copy.start()
+    for p in range(pieces):
+        dual_in(p).wait()
+        for k in range(ctgs):
+            tile_box[p, :, k, :] = dual_box[p, :, k * lines:(k + 1) * lines]
+        dual_out(p).start()
+    small_in[0].wait()
     lane = lax.broadcasted_iota(jnp.int32, (1, 128), 1) - lax.axis_index("ctg") * hour_rows
     for r in range(hour_rows):
-        out_price[r] = jnp.sum(jnp.where(lane == r, price[0:1], 0.0))
+        own_price[0:1, r:r + 1] = jnp.sum(
+            jnp.where(lane == r, price_box[0:1], 0.0), axis=1, keepdims=True
+        )
+    small_out[0].start()
+    for i in (1, 2):
+        small_in[i].wait()
+        small_out[i].start()
+    for p in range(pieces):
+        dual_out(p).wait()
+    for copy in small_out:
+        copy.wait()
 
 
 def body(
@@ -779,6 +864,7 @@
         out_specs=(hbm,) * 4,
         scratch_shapes=[
             pltpu.VMEM((chunks, flat, width), bf16),
+            pltpu.VMEM((chunks - 2, width, flat), bf16),
             pltpu.VMEM((chunks, gate_rows, width), f32),
             pltpu.VMEM(tile_pattern.shape, jnp.int32),
             pltpu.VMEM((gate_rows, tile_pattern.shape[2]), f32),
@@ -807,17 +893,14 @@
             pltpu.VMEM((chunks, hours, width), bf16),
             pltpu.VMEM((ITERS, chunks, hours, width), bf16),
             pltpu.VMEM((chunks, hours, width), bf16),
-            pltpu.VMEM((ITERS, chips, ROWS, width), bf16),
+            pltpu.VMEM((ITERS, n, ROWS, width), bf16),
             pltpu.VMEM((ITERS, chunks, hours, width), bf16),
             pltpu.VMEM((ITERS + 1, chips, 4, 128), f32),
             pltpu.VMEM((ITERS, 8, 128), f32),
             pltpu.VMEM((8, 128), f32),
             pltpu.VMEM((8, 128), f32),
-            sem((chunks,)), sem((13,)), sem((2 + 2 * chunks,)),
-            sem((chunks,)), sem((members,)), sem((members,)), sem((chunks,)),
-            sem((chunks,)), sem((chunks,)), sem((chips,)), sem((chips,)),
-            sem((n,)), sem((chips,)), sem((chips,)),
-            sem((2, chips)), sem((2, chips)),
+            sem((chunks,)), sem((members,)), sem((chunks,)), sem((chips,)), sem((n,)),
+            sem((n,)), sem((chips,)), sem((max(chips, chunks),)), sem((2, chips)),
             sem((6,)), sem((4,)),
         ],
         compiler_params=pltpu.CompilerParams(collective_id=0, has_side_effects=True),
@@ -837,17 +920,28 @@
         ramp_limit[None],
         ramp_mask[None],
     )
-    return pl.pallas_call(
+    levels, dual, ramp, price = pl.pallas_call(
         finish,
         out_shape=(
             jax.ShapeDtypeStruct((hour_rows, unit_count), f32),
             jax.ShapeDtypeStruct((hours, ctgs, lines), f32),
             jax.ShapeDtypeStruct((hour_rows, unit_count), f32),
-            jax.ShapeDtypeStruct((hour_rows,), f32),
+            jax.ShapeDtypeStruct((1, hour_rows), f32),
         ),
-        in_specs=[vmem] * 4,
-        out_specs=(vmem,) * 3 + (pl.BlockSpec(memory_space=pltpu.SMEM),),
+        in_specs=[hbm] * 4,
+        out_specs=(hbm,) * 4,
+        scratch_shapes=[
+            pltpu.VMEM((hour_rows, unit_count), f32),
+            pltpu.VMEM((hours // 8, 8, flat), f32),
+            pltpu.VMEM((hours // 8, 8, ctgs, lines), f32),
+            pltpu.VMEM((hour_rows, unit_count), f32),
+            pltpu.VMEM((8, 128), f32),
+            pltpu.VMEM((1, hour_rows), f32),
+            sem((3 + hours // 8,)),
+            sem((3 + hours // 8,)),
+        ],
     )(*out)
+    return levels, dual, ramp, price.reshape(hour_rows)
 
 
 def solution(mesh):

time: 72.2 us -> 65 us (0.900)
  Pallas kernels: 71.4 us -> 64.1 us
    pallas_call x1, Pallas kernels: 69.7 us -> 62.3 us  [body(): pl.pallas_call(functools.partial(kernel, n, hour_rows, step_size, balance...]
where the time goes in v2:
time: 65 us; the launch traced here: 64.8 us
  Pallas kernels  64.1 us (99%)
    pallas_call x1, Pallas kernels, body(): pl.pallas_call(functools.partial(kernel, n, hour_rows, step_size, balance...  62.3 us
    pallas_call x1, Pallas kernels, body(): pl.pallas_call(finish, out_shape=(jax.ShapeDtypeStruct((hour_rows, unit_c...  1.78 us

profile of v2, /device:TPU:0, one launch (start us, length us, event | category | flops | bytes accessed | tf_op | source)
XLA Modules:
  0.0 64.8 jit_solution(10300863215254462747)
XLA Ops:
  0.6 62.3 %shard_map.165 = (f32[2,3072]{1,0:T(2,128)}, f32[32,2048]{1,0:T(8,128)}, f32[2,3072]{1,0:T(2,128)}, f32[8,128]{1,0:T(8,128)}) custom-call(bf16[2048,3072]{1,0:T(8,128)(2,1)} %bitcast.8, s32[8,2,24]{2,1,0:T(2,128)} %pattern_hbm.1, s32[8,256]{1,0:T(8,128)} %index_hbm.1, f32[128,128]{1,0:T(8,128)} %bitcast.9, f32[32,8,256]{2,1,0:T(8,128)} %base_hbm.1, ...), custom_call_target="tpu_custom_call" | custom-call | tf_op jit(solution)/shard_map/pallas_call | solution.py:855
  63.0 1.8 %shard_map.166 = (f32[2,3072]{1,0:T(2,128)}, f32[32,8,256]{2,1,0:T(8,128)}, f32[2,3072]{1,0:T(2,128)}, f32[1,2]{1,0:T(1,128)}) custom-call(f32[2,3072]{1,0:T(2,128)} %get-tuple-element.12.levels, f32[32,2048]{1,0:T(8,128)} %get-tuple-element.13.dual, f32[2,3072]{1,0:T(2,128)} %get-tuple-element.14.ramp, f32[8,128]{1,0:T(8,128)} %get-tuple-element.15.price), custom_call_target="tpu_custom_call" | custom-call | tf_op jit(solution)/shard_map/pallas_call | solution.py:923

commit v3 on v2

--- a/solution.py
+++ b/solution.py
@@ -10,7 +10,7 @@
 
 ITERS = 4
 ROWS = 32
-STAT = 3
+STAT = 5
 LAG = 0
 AHEAD = 1
 IN_FLIGHT = 3
@@ -37,7 +37,7 @@
     start_stage, frag_in, frag_out,
     cost, levels, ramp, extended, halo_ext, halo_ramp,
     pull_out, pair_in, pull_sum, pull_in, ext_half, stats, flow_stat, price, omega,
-    frag_send, frag_recv, pair_recv, pull_send, pull_recv, ext_send, ext_recv, stat_send, stat_recv,
+    frag_send, frag_recv, pull_send, pull_recv, ext_send, ext_recv, stat_send, stat_recv,
     core_sems, halo_sems,
 ):
     f32 = jnp.float32
@@ -92,7 +92,7 @@
         return (j >= EARLY) == owner
 
     def both_cores(c):
-        return lax.div(c, 2) == my_pair
+        return c == my_chunk
 
     def block_rows(g):
         return pl.ds(pl.multiple_of(g * ROWS, ROWS), ROWS)
@@ -189,7 +189,7 @@
         return send(price, price, core_sems.at[4], core_sems.at[5], partner)
 
     def pair_copy(it, c):
-        return send(pull_out.at[c], pair_in.at[it, c], pull_send.at[c * groups], pair_recv.at[c], partner)
+        return send(pull_out.at[c], pair_in.at[it, c], pull_send.at[c * groups], pull_recv.at[c], partner)
 
     def pull_copy(it, src, target_chip, sender):
         c, g = lax.div(target_chip, groups), lax.rem(target_chip, groups)
@@ -603,6 +603,16 @@
         small_out(1).start()
         small_out(2).start()
 
+    turns = (chunks - 1) // 2
+    blocks = ctgs * lines // 256
+
+    def turn(first, last):
+        @pl.loop(first * blocks, last * blocks)
+        def _(i):
+            j = lax.div(i, blocks)
+            block = pl.ds(pl.multiple_of(lax.rem(i, blocks) * 256, 256), 256)
+            turned[j, :, block] = masked[far_chunk(j), block, :].T
+
     @pl.loop(0, ITERS)
     def _(it):
         @pl.when(it > 0)
@@ -621,15 +631,9 @@
 
                 forward(it, j - LAG)
 
-            turn = (chunks - 1) // 2
-
             @pl.when(it < 3)
             def _():
-                @pl.loop(0, turn * (ctgs * lines // 256))
-                def _(i):
-                    j = (it - 1) * turn + lax.div(i, ctgs * lines // 256)
-                    block = pl.ds(pl.multiple_of(lax.rem(i, ctgs * lines // 256) * 256, 256), 256)
-                    turned[j, :, block] = masked[far_chunk(j), block, :].T
+                turn((it - 1) * turns, (it - 1) * turns + turns - 1)
 
         pull_sent(it)
 
@@ -644,8 +648,12 @@
         def _():
             line_limits()
 
+        @pl.when((it > 0) & (it < 3))
+        def _():
+            turn(it * turns - 1, it * turns)
+
         near = my_pair * 2 + 1 - my_side
-        take(it, near)
+        take_and_pass(it, near)
         flow_acc[...] += flow(ext_half[it, near], masked[near])
 
         @pl.loop(1, pairs + AHEAD)
@@ -899,7 +907,7 @@
             pltpu.VMEM((ITERS, 8, 128), f32),
             pltpu.VMEM((8, 128), f32),
             pltpu.VMEM((8, 128), f32),
-            sem((chunks,)), sem((members,)), sem((chunks,)), sem((chips,)), sem((n,)),
+            sem((chunks,)), sem((members,)), sem((chips,)), sem((n,)),
             sem((n,)), sem((chips,)), sem((max(chips, chunks),)), sem((2, chips)),
             sem((6,)), sem((4,)),
         ],

time: 65 us -> 63.3 us (0.974)
  Pallas kernels: 64.1 us -> 62.4 us
    pallas_call x1, Pallas kernels: 62.3 us -> 60.6 us  [body(): pl.pallas_call(functools.partial(kernel, n, hour_rows, step_size, balance...]
where the time goes in v3:
time: 63.3 us; the launch traced here: 63 us
  Pallas kernels  62.4 us (99%)
  between operations  0.64 us (1%)
    pallas_call x1, Pallas kernels, body(): pl.pallas_call(functools.partial(kernel, n, hour_rows, step_size, balance...  60.6 us
    pallas_call x1, Pallas kernels, body(): pl.pallas_call(finish, out_shape=(jax.ShapeDtypeStruct((hour_rows, unit_c...  1.78 us

profile of v3, /device:TPU:0, one launch (start us, length us, event | category | flops | bytes accessed | tf_op | source)
XLA Modules:
  0.0 63.0 jit_solution(15612692899040430543)
XLA Ops:
  0.6 60.6 %shard_map.165 = (f32[2,3072]{1,0:T(2,128)}, f32[32,2048]{1,0:T(8,128)}, f32[2,3072]{1,0:T(2,128)}, f32[8,128]{1,0:T(8,128)}) custom-call(bf16[2048,3072]{1,0:T(8,128)(2,1)} %bitcast.8, s32[8,2,24]{2,1,0:T(2,128)} %pattern_hbm.1, s32[8,256]{1,0:T(8,128)} %index_hbm.1, f32[128,128]{1,0:T(8,128)} %bitcast.9, f32[32,8,256]{2,1,0:T(8,128)} %base_hbm.1, ...), custom_call_target="tpu_custom_call" | custom-call | tf_op jit(solution)/shard_map/pallas_call | solution.py:863
  61.3 1.8 %shard_map.166 = (f32[2,3072]{1,0:T(2,128)}, f32[32,8,256]{2,1,0:T(8,128)}, f32[2,3072]{1,0:T(2,128)}, f32[1,2]{1,0:T(1,128)}) custom-call(f32[2,3072]{1,0:T(2,128)} %get-tuple-element.12.levels, f32[32,2048]{1,0:T(8,128)} %get-tuple-element.13.dual, f32[2,3072]{1,0:T(2,128)} %get-tuple-element.14.ramp, f32[8,128]{1,0:T(8,128)} %get-tuple-element.15.price), custom_call_target="tpu_custom_call" | custom-call | tf_op jit(solution)/shard_map/pallas_call | solution.py:931

commit v4 on v3

--- a/solution.py
+++ b/solution.py
@@ -633,7 +633,11 @@
 
             @pl.when(it < 3)
             def _():
-                turn((it - 1) * turns, (it - 1) * turns + turns - 1)
+                turn(1 + (it - 1) * turns, it * turns)
+
+        @pl.when(it == 0)
+        def _():
+            turn(0, 1)
 
         pull_sent(it)
 
@@ -648,9 +652,9 @@
         def _():
             line_limits()
 
-        @pl.when((it > 0) & (it < 3))
-        def _():
-            turn(it * turns - 1, it * turns)
+        @pl.when(it == 1)
+        def _():
+            turn(turns, turns + 1)
 
         near = my_pair * 2 + 1 - my_side
         take_and_pass(it, near)
@@ -673,7 +677,7 @@
                 place = (pairs - 1 - j + AHEAD) * 2
                 c, d = far_chunk(place), far_chunk(place + 1)
                 x = jnp.concatenate([ext_half[it, c], ext_half[it, d]], axis=1)
-                ready = (it > 1) | ((it == 1) & (place + 1 < (chunks - 1) // 2))
+                ready = (it > 1) | ((it == 1) & (place <= turns - 1))
 
                 @pl.when(ready)
                 def _():

time: 63.3 us -> 62.4 us (0.986)
  Pallas kernels: 62.4 us -> 61.5 us
    pallas_call x1, Pallas kernels: 60.6 us -> 59.7 us  [body(): pl.pallas_call(functools.partial(kernel, n, hour_rows, step_size, balance...]
where the time goes in v4:
time: 62.4 us; the launch traced here: 62.2 us
  Pallas kernels  61.5 us (99%)
  between operations  0.64 us (1%)
    pallas_call x1, Pallas kernels, body(): pl.pallas_call(functools.partial(kernel, n, hour_rows, step_size, balance...  59.7 us
    pallas_call x1, Pallas kernels, body(): pl.pallas_call(finish, out_shape=(jax.ShapeDtypeStruct((hour_rows, unit_c...  1.78 us

profile of v4, /device:TPU:0, one launch (start us, length us, event | category | flops | bytes accessed | tf_op | source)
XLA Modules:
  0.0 62.2 jit_solution(5167308223261374467)
XLA Ops:
  0.6 59.7 %shard_map.165 = (f32[2,3072]{1,0:T(2,128)}, f32[32,2048]{1,0:T(8,128)}, f32[2,3072]{1,0:T(2,128)}, f32[8,128]{1,0:T(8,128)}) custom-call(bf16[2048,3072]{1,0:T(8,128)(2,1)} %bitcast.8, s32[8,2,24]{2,1,0:T(2,128)} %pattern_hbm.1, s32[8,256]{1,0:T(8,128)} %index_hbm.1, f32[128,128]{1,0:T(8,128)} %bitcast.9, f32[32,8,256]{2,1,0:T(8,128)} %base_hbm.1, ...), custom_call_target="tpu_custom_call" | custom-call | tf_op jit(solution)/shard_map/pallas_call | solution.py:867
  60.4 1.8 %shard_map.166 = (f32[2,3072]{1,0:T(2,128)}, f32[32,8,256]{2,1,0:T(8,128)}, f32[2,3072]{1,0:T(2,128)}, f32[1,2]{1,0:T(1,128)}) custom-call(f32[2,3072]{1,0:T(2,128)} %get-tuple-element.12.levels, f32[32,2048]{1,0:T(8,128)} %get-tuple-element.13.dual, f32[2,3072]{1,0:T(2,128)} %get-tuple-element.14.ramp, f32[8,128]{1,0:T(8,128)} %get-tuple-element.15.price), custom_call_target="tpu_custom_call" | custom-call | tf_op jit(solution)/shard_map/pallas_call | solution.py:935

commit v5 on v4

--- a/solution.py
+++ b/solution.py
@@ -631,9 +631,13 @@
 
                 forward(it, j - LAG)
 
-            @pl.when(it < 3)
-            def _():
-                turn(1 + (it - 1) * turns, it * turns)
+            @pl.when(it == 1)
+            def _():
+                turn(1, turns)
+
+            @pl.when(it == 2)
+            def _():
+                turn(turns + 1, 2 * turns - 1)
 
         @pl.when(it == 0)
         def _():
@@ -655,6 +659,10 @@
         @pl.when(it == 1)
         def _():
             turn(turns, turns + 1)
+
+        @pl.when(it == 2)
+        def _():
+            turn(2 * turns - 1, 2 * turns)
 
         near = my_pair * 2 + 1 - my_side
         take_and_pass(it, near)

time: 62.4 us -> 62.4 us (level)
  no operation moved by 1% of the time
where the time goes in v5:
time: 62.4 us; the launch traced here: 62.2 us
  Pallas kernels  61.5 us (99%)
  between operations  0.64 us (1%)
    pallas_call x1, Pallas kernels, body(): pl.pallas_call(functools.partial(kernel, n, hour_rows, step_size, balance...  59.7 us
    pallas_call x1, Pallas kernels, body(): pl.pallas_call(finish, out_shape=(jax.ShapeDtypeStruct((hour_rows, unit_c...  1.78 us

profile of v5, /device:TPU:0, one launch (start us, length us, event | category | flops | bytes accessed | tf_op | source)
XLA Modules:
  0.0 62.2 jit_solution(15307937856294509961)
XLA Ops:
  0.6 59.7 %shard_map.165 = (f32[2,3072]{1,0:T(2,128)}, f32[32,2048]{1,0:T(8,128)}, f32[2,3072]{1,0:T(2,128)}, f32[8,128]{1,0:T(8,128)}) custom-call(bf16[2048,3072]{1,0:T(8,128)(2,1)} %bitcast.8, s32[8,2,24]{2,1,0:T(2,128)} %pattern_hbm.1, s32[8,256]{1,0:T(8,128)} %index_hbm.1, f32[128,128]{1,0:T(8,128)} %bitcast.9, f32[32,8,256]{2,1,0:T(8,128)} %base_hbm.1, ...), custom_call_target="tpu_custom_call" | custom-call | tf_op jit(solution)/shard_map/pallas_call | solution.py:875
  60.4 1.8 %shard_map.166 = (f32[2,3072]{1,0:T(2,128)}, f32[32,8,256]{2,1,0:T(8,128)}, f32[2,3072]{1,0:T(2,128)}, f32[1,2]{1,0:T(1,128)}) custom-call(f32[2,3072]{1,0:T(2,128)} %get-tuple-element.12.levels, f32[32,2048]{1,0:T(8,128)} %get-tuple-element.13.dual, f32[2,3072]{1,0:T(2,128)} %get-tuple-element.14.ramp, f32[8,128]{1,0:T(8,128)} %get-tuple-element.15.price), custom_call_target="tpu_custom_call" | custom-call | tf_op jit(solution)/shard_map/pallas_call | solution.py:943

commit v6 on v4

--- a/solution.py
+++ b/solution.py
@@ -656,9 +656,22 @@
         def _():
             turn(turns, turns + 1)
 
+        @pl.when(it == 2)
+        def _():
+            turn(2 * turns, 2 * turns + 1)
+
         near = my_pair * 2 + 1 - my_side
         take_and_pass(it, near)
-        flow_acc[...] += flow(ext_half[it, near], masked[near])
+
+        @pl.when(it < 2)
+        def _():
+            flow_acc[...] += flow(ext_half[it, near], masked[near])
+
+        @pl.when(it > 1)
+        def _():
+            flow_acc[...] += jnp.dot(
+                ext_half[it, near], turned[2 * turns], preferred_element_type=f32
+            )
 
         @pl.loop(1, pairs + AHEAD)
         def _(j):
@@ -876,7 +889,7 @@
         out_specs=(hbm,) * 4,
         scratch_shapes=[
             pltpu.VMEM((chunks, flat, width), bf16),
-            pltpu.VMEM((chunks - 2, width, flat), bf16),
+            pltpu.VMEM((chunks - 1, width, flat), bf16),
             pltpu.VMEM((chunks, gate_rows, width), f32),
             pltpu.VMEM(tile_pattern.shape, jnp.int32),
             pltpu.VMEM((gate_rows, tile_pattern.shape[2]), f32),

time: 62.4 us -> 62.4 us (level)
  no operation moved by 1% of the time
where the time goes in v6:
time: 62.4 us; the launch traced here: 62.2 us
  Pallas kernels  61.5 us (99%)
  between operations  0.64 us (1%)
    pallas_call x1, Pallas kernels, body(): pl.pallas_call(functools.partial(kernel, n, hour_rows, step_size, balance...  59.7 us
    pallas_call x1, Pallas kernels, body(): pl.pallas_call(finish, out_shape=(jax.ShapeDtypeStruct((hour_rows, unit_c...  1.78 us

profile of v6, /device:TPU:0, one launch (start us, length us, event | category | flops | bytes accessed | tf_op | source)
XLA Modules:
  0.0 62.2 jit_solution(16417760891493306014)
XLA Ops:
  0.6 59.7 %shard_map.165 = (f32[2,3072]{1,0:T(2,128)}, f32[32,2048]{1,0:T(8,128)}, f32[2,3072]{1,0:T(2,128)}, f32[8,128]{1,0:T(8,128)}) custom-call(bf16[2048,3072]{1,0:T(8,128)(2,1)} %bitcast.8, s32[8,2,24]{2,1,0:T(2,128)} %pattern_hbm.1, s32[8,256]{1,0:T(8,128)} %index_hbm.1, f32[128,128]{1,0:T(8,128)} %bitcast.9, f32[32,8,256]{2,1,0:T(8,128)} %base_hbm.1, ...), custom_call_target="tpu_custom_call" | custom-call | tf_op jit(solution)/shard_map/pallas_call | solution.py:880
  60.4 1.8 %shard_map.166 = (f32[2,3072]{1,0:T(2,128)}, f32[32,8,256]{2,1,0:T(8,128)}, f32[2,3072]{1,0:T(2,128)}, f32[1,2]{1,0:T(1,128)}) custom-call(f32[2,3072]{1,0:T(2,128)} %get-tuple-element.12.levels, f32[32,2048]{1,0:T(8,128)} %get-tuple-element.13.dual, f32[2,3072]{1,0:T(2,128)} %get-tuple-element.14.ramp, f32[8,128]{1,0:T(8,128)} %get-tuple-element.15.price), custom_call_target="tpu_custom_call" | custom-call | tf_op jit(solution)/shard_map/pallas_call | solution.py:948
